TPU v7x, 32 devices: a whole 2x2x4 slice. The times are simulated.
32 devices in a mesh: row: 16 (over z, y, core), col: 2 (over x).
Axes of the slice: x: 2, y: 2, z: 4, core: 2. Of those that a mesh axis runs over, the one named last changes fastest.
Arguments:
- row_embed: bfloat16 [300, 16384], P(None, 'row'), may hold values from -1.796875 to 1.796875
- col_embed: bfloat16 [300, 2, 256], P(None, 'col', 'row'), may hold values from -1.796875 to 1.796875
- counts: int32 [16384, 2, 256], P('row', 'col'), may hold values from 0 to 64, as said below
- occupancy: int32 [128, 2, 2], P('row', 'col'), may hold values from 0 to 1, as said below
- row_marg: int32 [16384], P('row'), may hold values from 2000 to 199999
- col_marg: int32 [2, 256], P('col', 'row'), may hold values from 2000 to 199999
- log_total: float32 [1], replicated, may hold values from 18 to 22
Outputs:
- grad_rows: float32 [300, 16384], P(None, 'row')
- grad_cols: float32 [300, 2, 256], P(None, 'col', 'row')
Inputs may be any that keep to these rules, and one draw needn't show every extreme that they name: counts of the band's cells; zero in part of the cells. `occupancy`: the share of tiles marked 1 differs from row tile to row tile.
All inputs are finite; a program needn't handle non-finite values.
Results may differ from a plain program's by a relative error of at most 0.0018.
Values may be sent and summed in bfloat16 or wider, within the bound.
A program may use at most 64 MiB of HBM per device.

v0:
```python
import functools
import math

import jax
import jax.numpy as jnp
from jax import lax
from jax.experimental import pallas as pl
from jax.experimental.pallas import tpu as pltpu
from jax.sharding import PartitionSpec as P

LANES = 128
SEND = jnp.bfloat16


def nt(a, b):
    return lax.dot_general(a, b, (((1,), (1,)), ((), ())), preferred_element_type=jnp.float32)


def nn(a, b):
    return lax.dot_general(a, b, (((1,), (0,)), ((), ())), preferred_element_type=jnp.float32)


def split3(x):
    hi = x.astype(jnp.bfloat16).astype(jnp.float32)
    rest = x - hi
    mid = rest.astype(jnp.bfloat16).astype(jnp.float32)
    return hi, mid, rest - mid


def eye(n):
    r = lax.broadcasted_iota(jnp.int32, (n, n), 0)
    c = lax.broadcasted_iota(jnp.int32, (n, n), 1)
    return (r == c).astype(jnp.float32).astype(jnp.bfloat16)


def slope_terms(code):
    slope = jnp.where(code > 0.0, 0.1 + 0.25 * jnp.sqrt(jnp.maximum(code, 0.0)), 0.0)
    return slope, jnp.log(jnp.maximum(code, 1.0))


def cell(code, slope, logc, gap):
    return jnp.where(code == 0.0, jax.nn.sigmoid(gap), slope * (gap - logc))


def repeat(n, fn):
    if n == 1:
        fn(0)
    else:
        pl.loop(0, n)(fn)


def kernel(cfg, r_hbm, c_hbm, cnt_hbm, occ_hbm, rm_hbm, cm_hbm, lt_ref,
           rows_out, cols_out,
           r_v, cnt_v, raug, blk, cg, cd, enc, slope_v, logc_v, res, gcol, s1buf, s2src, s2buf,
           c_ref, occ_ref, rm_ref, cm_ref, dsem, gz_s, gz_r, gc_s, gc_r, gx_s, gx_r, e_s, e_r, a_s, a_r, b_s, b_r, token):
    n, d, dp, w, band, rows, tile, q_w, scale_r, scale_c = cfg
    half = n // 2
    nq = rows // q_w
    btiles = band // LANES
    sub = min(band, 256)
    nsub = band // sub
    me = lax.axis_index("row")
    col = lax.axis_index("col")
    core = lax.rem(me, 2)
    mate = me + 1 - 2 * core
    mine = me // 2
    peers = [lax.rem(me + 2 * k, n) for k in range(1, half)]
    froms = [lax.rem(me - 2 * k + n, n) for k in range(1, half)]
    at_mate = (mate, col)
    at_x = (me, 1 - col)

    def rcopy(src, dst, ss, rs, dev):
        return pltpu.make_async_remote_copy(
            src_ref=src, dst_ref=dst, send_sem=ss, recv_sem=rs,
            device_id=dev, device_id_type=pl.DeviceIdType.MESH)

    barrier = pltpu.get_barrier_semaphore()
    masks = [half >> k for k in range(1, half.bit_length())]
    near = [(2 * (mine + m - 2 * m * lax.rem(mine // m, 2)) + core, col) for m in masks]
    for dev in near + [at_mate, at_x]:
        pl.semaphore_signal(barrier, inc=1, device_id=dev, device_id_type=pl.DeviceIdType.MESH)
    small = []
    for k, (src, dst) in enumerate(((cm_hbm, cm_ref), (c_hbm, c_ref), (occ_hbm, occ_ref),
                                    (rm_hbm, rm_ref))):
        cp = pltpu.make_async_copy(src, dst, dsem.at[nq + 1 + k])
        cp.start()
        small.append(cp)
    step = q_w * btiles
    loads = []
    for q in range(nq):
        cp = pltpu.make_async_copy(
            cnt_hbm.at[pl.ds(q * step, step), :], cnt_v.at[pl.ds(q * step, step), :], dsem.at[q])
        cp.start()
        loads.append(cp)
    rload = pltpu.make_async_copy(r_hbm, r_v, dsem.at[nq])
    rload.start()

    for cp in small:
        cp.wait()

    log_c = jnp.log(cm_ref[...].astype(jnp.float32))
    ri = lax.broadcasted_iota(jnp.int32, (w, w), 0)
    ci = lax.broadcasted_iota(jnp.int32, (w, w), 1)
    log_c = jnp.sum(jnp.where(ri == ci, jnp.broadcast_to(log_c, (w, w)), 0.0), axis=1, keepdims=True)
    hi, mid, lo = split3(log_c)
    blk[...] = jnp.zeros_like(blk)
    blk[:, pl.ds(0, d)] = c_ref[...].astype(jnp.float32)
    li = lax.broadcasted_iota(jnp.int32, (w, dp), 1)
    own = blk[...]
    for at, val in ((d, hi), (d + 1, mid), (d + 2, lo)):
        own = jnp.where(li == at, val, own)
    own = jnp.where((li >= d + 3) & (li < d + 6), 1.0, own)
    cg[0, me] = own.astype(jnp.bfloat16)

    ident = eye(LANES)

    def encode(q):
        loads[q].wait()

        def part(t):
            cells = []
            for u in range(q_w // tile):
                x = cnt_v[pl.ds(q * step + u * tile * btiles + t, tile, stride=btiles), :]
                k = q * (q_w // tile) + u
                on = jnp.broadcast_to(occ_ref[t:t + 1, k:k + 1], (tile, LANES)) != 0
                cells.append(jnp.where(on, x, -1).astype(jnp.float32).astype(jnp.bfloat16))
            code = nt(ident, jnp.concatenate(cells, axis=0))
            at = pl.ds(t * LANES, LANES)
            enc[0, q, at, :] = code.astype(jnp.bfloat16)
            slope_v[q, at, :], logc_v[q, at, :] = slope_terms(code)

        for t in range(btiles):
            part(t)

    ecopies = [rcopy(enc.at[0, q], enc.at[1, q], e_s.at[q], e_r.at[q], at_x) for q in range(nq)]
    encode(0)
    pl.semaphore_wait(barrier, len(masks) + 2)
    ecopies[0].start()
    xcp = rcopy(cg.at[0, me], cg.at[1, me], gx_s, gx_r, at_x)
    xcp.start()
    sends = [xcp]
    cp = rcopy(cg.at[0, me], cg.at[0, me], gc_s.at[0, mine], gc_r.at[0, mine], at_mate)
    cp.start()
    sends.append(cp)

    done = 1
    for k in range(1, len(masks)):
        pl.semaphore_signal(token.at[k], inc=1, device_id=near[k], device_id_type=pl.DeviceIdType.MESH)
        if done < nq:
            encode(done)
        pl.semaphore_wait(token.at[k], 1)
        if done < nq:
            ecopies[done].start()
            done += 1

    for p in peers:
        cp = rcopy(cg.at[0, me], cg.at[0, me], gz_s.at[0, p // 2], gz_r.at[0, mine], (p, col))
        cp.start()
        sends.append(cp)
    for q in range(done, nq):
        encode(q)
        if q > done:
            ecopies[q - 1].start()

    xcp.wait_recv()
    for p in peers:
        cp = rcopy(cg.at[1, me], cg.at[1, me], gz_s.at[1, p // 2], gz_r.at[1, mine], (p, col))
        cp.start()
        sends.append(cp)
    cp = rcopy(cg.at[1, me], cg.at[1, me], gc_s.at[1, mine], gc_r.at[1, mine], at_mate)
    cp.start()
    sends.append(cp)

    if done < nq:
        ecopies[nq - 1].start()

    rload.wait()
    raug[pl.ds(0, d), :] = r_v[...]
    first = (d // 16) * 16
    row_term = jnp.log(rm_ref[...].astype(jnp.float32)) - lt_ref[0]
    hi, mid, lo = split3(row_term)
    tail = raug[pl.ds(first, dp - first), :].astype(jnp.float32)
    si = lax.broadcasted_iota(jnp.int32, (dp - first, rows), 0) + first
    tail = jnp.where(si < d, tail, jnp.where(si < d + 3, 1.0, 0.0))
    for at, val in ((d + 3, hi), (d + 4, mid), (d + 5, lo)):
        tail = jnp.where(si == at, val, tail)
    raug[pl.ds(first, dp - first), :] = tail.astype(jnp.bfloat16)

    def forward(which):
        for p in froms:
            rcopy(cg.at[which, p], cg.at[which, p], gz_s.at[which, p // 2],
                  gz_r.at[which, p // 2], at_mate).wait_recv()
            cp = rcopy(cg.at[which, p], cg.at[which, p], gc_s.at[which, p // 2],
                       gc_r.at[which, p // 2], at_mate)
            cp.start()
            sends.append(cp)

    def mate_blocks(which):
        for k in range(half):
            at = 2 * k + 1 - core
            rcopy(cg.at[which, at], cg.at[which, at], gc_s.at[which, k],
                  gc_r.at[which, k], at_mate).wait_recv()

    forward(0)
    mate_blocks(0)

    per = sub // w

    def block(which, s):
        return cg[which, pl.ds(s * per, per)].reshape(sub, dp)

    for q in range(nq):
        qs = pl.ds(q * q_w, q_w)

        def cells(s):
            at = pl.ds(s * sub, sub)
            gap = nn(block(0, s), raug[:, qs])
            code = enc[0, q, at, :].astype(jnp.float32)
            res[at, qs] = cell(code, slope_v[q, at, :], logc_v[q, at, :], gap).astype(jnp.bfloat16)

        repeat(nsub, cells)

    def col_terms(s):
        gcol[pl.ds(s * per, per)] = nt(res[pl.ds(s * sub, sub), :], raug[...]).reshape(per, w, dp)

    repeat(nsub, col_terms)
    for p in peers + [me]:
        k = p // 2
        cp = rcopy(gcol.at[2 * k + 1 - core], s1buf.at[k], a_s.at[k], a_r.at[k], at_mate)
        cp.start()
        sends.append(cp)

    ident_d = eye(dp)

    def transposed(which):
        def one(s):
            cd[which, :, pl.ds(s * sub, sub)] = nt(ident_d, block(which, s)).astype(jnp.bfloat16)

        repeat(nsub, one)

    transposed(0)
    rows_out[...] = nn(cd[0], res[...])[:d, :]

    held = None
    for p in peers + [me]:
        rcopy(gcol.at[p], s1buf.at[p // 2], a_s.at[p // 2], a_r.at[p // 2], at_mate).wait_recv()
        if p is me:
            total = gcol[me] + s1buf[mine]
        else:
            s2src[p // 2] = (gcol[p] + s1buf[p // 2]).astype(s2src.dtype)
        if held is not None:
            held.start()
            sends.append(held)
        held = None if p is me else rcopy(
            s2src.at[p // 2], s2buf.at[mine], b_s.at[p // 2], b_r.at[mine], (p, col))

    forward(1)
    mate_blocks(1)
    transposed(1)
    for q in range(nq):
        qs = pl.ds(q * q_w, q_w)
        ecopies[q].wait_recv()

        def cells(s):
            at = pl.ds(s * sub, sub)
            gap = nn(block(1, s), raug[:, qs])
            code = enc[1, q, at, :].astype(jnp.float32)
            slope, logc = slope_terms(code)
            res[at, qs] = cell(code, slope, logc, gap).astype(jnp.bfloat16)

        repeat(nsub, cells)
        rows_out[:, qs] = (rows_out[:, qs] + nn(cd[1], res[:, qs])[:d, :]) * scale_r

    for p in froms:
        rcopy(s2src.at[0], s2buf.at[p // 2], b_s.at[p // 2], b_r.at[p // 2], at_mate).wait_recv()
        total = total + s2buf[p // 2].astype(jnp.float32)
    cols_out[...] = (total * scale_c)[:, :d]
    for cp in sends + ecopies:
        cp.wait_send()


def scratch_bytes(shapes):
    return sum(math.prod(s.shape) * jnp.dtype(s.dtype).itemsize for s in shapes)


def place(rows_in, cols_in, rows_out, cols_out, sem):
    copies = [pltpu.make_async_copy(rows_in, rows_out, sem.at[0]),
              pltpu.make_async_copy(cols_in, cols_out, sem.at[1])]
    for cp in copies:
        cp.start()
    for cp in copies:
        cp.wait()


def body(row_embed, col_embed, counts, occupancy, row_marg, col_marg, log_total):
    n = lax.axis_size("row")
    d, rows = row_embed.shape
    w = col_embed.shape[2]
    band = counts.shape[2]
    tile = rows // occupancy.shape[0]
    q_w = 2 * tile if rows % (2 * tile) == 0 else tile
    dp = -(-(d + 6) // LANES) * LANES
    half = n // 2
    nq = rows // q_w
    btiles = band // LANES
    cfg = (n, d, dp, w, band, rows, tile, q_w,
           1.0 / math.sqrt(w * n * lax.axis_size("col")), 1.0 / math.sqrt(rows * n))
    bf, f32 = jnp.bfloat16, jnp.float32
    vm, hb, anywhere = (pl.BlockSpec(memory_space=m) for m in (pltpu.VMEM, pltpu.HBM, pl.ANY))
    dma = lambda *s: pltpu.SemaphoreType.DMA(s) if s else pltpu.SemaphoreType.DMA
    scratch = [
        pltpu.VMEM((d, rows), bf),
        pltpu.VMEM((rows * btiles, LANES), jnp.int32),
        pltpu.VMEM((dp, rows), bf),
        pltpu.VMEM((w, dp), f32),
        pltpu.VMEM((2, n, w, dp), bf),
        pltpu.VMEM((2, dp, band), bf),
        pltpu.VMEM((2, nq, band, q_w), bf),
        pltpu.VMEM((nq, band, q_w), f32),
        pltpu.VMEM((nq, band, q_w), f32),
        pltpu.VMEM((band, rows), bf),
        pltpu.VMEM((n, w, dp), f32),
        pltpu.VMEM((half, w, dp), f32),
        pltpu.VMEM((half, w, dp), SEND),
        pltpu.VMEM((half, w, dp), SEND),
        pltpu.VMEM((w, d), bf),
        pltpu.VMEM((occupancy.shape[2], occupancy.shape[0]), jnp.int32),
        pltpu.VMEM((1, rows), jnp.int32),
        pltpu.VMEM((1, w), jnp.int32),
        dma(nq + 5),
        dma(2, half), dma(2, half), dma(2, half), dma(2, half), dma(), dma(),
        dma(nq), dma(nq), dma(half), dma(half), dma(half), dma(half),
        pltpu.SemaphoreType.REGULAR((half.bit_length() - 1,)),
    ]
    limit = min(60 << 20, (6 << 20) + scratch_bytes(scratch[:18]) + 2 * d * rows * 4 + 24 * band * q_w)
    grad_rows, grad_cols = pl.pallas_call(
        functools.partial(kernel, cfg),
        out_shape=(jax.ShapeDtypeStruct((d, rows), f32), jax.ShapeDtypeStruct((w, d), f32)),
        in_specs=[hb] * 6 + [pl.BlockSpec(memory_space=pltpu.SMEM)],
        out_specs=(vm, vm),
        scratch_shapes=scratch,
        compiler_params=pltpu.CompilerParams(
            collective_id=0, has_side_effects=True, vmem_limit_bytes=limit),
    )(
        *(pltpu.with_memory_space_constraint(x, pltpu.HBM) for x in (
            row_embed,
            jnp.transpose(col_embed, (1, 2, 0)).reshape(w, d),
            counts.reshape(rows * btiles, LANES),
            jnp.transpose(occupancy, (1, 2, 0)).reshape(occupancy.shape[2], occupancy.shape[0]),
            row_marg.reshape(1, rows),
            col_marg,
        )),
        log_total,
    )
    grad_rows, grad_cols = pl.pallas_call(
        place,
        out_shape=(jax.ShapeDtypeStruct((d, rows), f32), jax.ShapeDtypeStruct((w, d), f32)),
        in_specs=[anywhere, anywhere],
        out_specs=(hb, hb),
        scratch_shapes=[pltpu.SemaphoreType.DMA((2,))],
    )(*(pltpu.with_memory_space_constraint(x, pltpu.VMEM) for x in (grad_rows, grad_cols)))
    return grad_rows, jnp.transpose(grad_cols.reshape(1, w, d), (2, 0, 1))


def solution(mesh):
    placed = (
        P(None, "row"),
        P(None, "col", "row"),
        P("row", "col", None),
        P("row", "col", None),
        P("row"),
        P("col", "row"),
        P(),
    )
    return jax.shard_map(
        body,
        mesh=mesh,
        in_specs=placed,
        out_specs=(P(None, "row"), P(None, "col", "row")),
        check_vma=False,
    )
```

profile of v0, /device:TPU:0, one launch (start us, length us, event | category | flops | bytes accessed | tf_op | source)
XLA Modules:
  0.0 23.1 jit_solution(12481788627422227711)
XLA Ops:
  1.3 20.7 %shard_map.86 = (f32[300,1024]{1,0:T(8,128)S(1)}, f32[16,300]{1,0:T(8,128)S(1)}) custom-call(bf16[300,1024]{1,0:T(8,128)(2,1)} %r_hbm.1, bf16[16,300]{1,0:T(8,128)(2,1)} %bitcast.12, s32[2048,128]{1,0:T(8,128)} %bitcast.11, s32[2,8]{1,0:T(2,128)} %bitcast.14, s32[1,1024]{1,0:T(1,128)} %bitcast.13, s32[1,16]{1,0:T(1,128)} %cm_hbm.1, f32[1]{0:T(128)S(6)} %copy.9.lt_ref), custom_call_target="tpu_custom_call" | custom-call | tf_op jit(solution)/shard_map/pallas_call | solution.py:336
  22.0 1.1 %shard_map.87 = (f32[300,1024]{1,0:T(8,128)}, f32[16,300]{1,0:T(8,128)}) custom-call(f32[300,1024]{1,0:T(8,128)S(1)} %get-tuple-element.6.rows_in, f32[16,300]{1,0:T(8,128)S(1)} %get-tuple-element.7.cols_in), custom_call_target="tpu_custom_call" | custom-call | tf_op jit(solution)/shard_map/pallas_call | solution.py:355
where the time goes:
time: 23.2 us; the launch traced here: 23.1 us
  Pallas kernels  21.8 us (94%)
  between operations  1.29 us (6%)
    pallas_call x1, Pallas kernels, body(): pl.pallas_call(functools.partial(kernel, cfg), out_shape=(jax.ShapeDtypeS...  20.7 us
    pallas_call x1, Pallas kernels, body(): pl.pallas_call(place, out_shape=(jax.ShapeDtypeStruct((d, rows), f32), ja...  1.06 us

commit v1 on v0

--- a/solution.py
+++ b/solution.py
@@ -52,49 +52,86 @@
 def kernel(cfg, r_hbm, c_hbm, cnt_hbm, occ_hbm, rm_hbm, cm_hbm, lt_ref,
            rows_out, cols_out,
            r_v, cnt_v, raug, blk, cg, cd, enc, slope_v, logc_v, res, gcol, s1buf, s2src, s2buf,
-           c_ref, occ_ref, rm_ref, cm_ref, dsem, gz_s, gz_r, gc_s, gc_r, gx_s, gx_r, e_s, e_r, a_s, a_r, b_s, b_r, token):
+           c_ref, occ_ref, rm_ref, cm_ref, dsem, e_s, e_r, gx_s, gx_r, g_s, g_r, w_r, m_s, m_r,
+           a_s, a_r, b_s, b_r, token):
     n, d, dp, w, band, rows, tile, q_w, scale_r, scale_c = cfg
     half = n // 2
+    hh = half // 2
     nq = rows // q_w
     btiles = band // LANES
     sub = min(band, 256)
     nsub = band // sub
+    gcols = band // 2
+    subg = min(gcols, 256)
+    nsubg = gcols // subg
     me = lax.axis_index("row")
     col = lax.axis_index("col")
     core = lax.rem(me, 2)
     mate = me + 1 - 2 * core
     mine = me // 2
-    peers = [lax.rem(me + 2 * k, n) for k in range(1, half)]
-    froms = [lax.rem(me - 2 * k + n, n) for k in range(1, half)]
+    own_half = mine // hh
+    halves = (own_half, 1 - own_half)
+    froms = [lax.rem(mine - k + half, half) for k in range(1, half)]
     at_mate = (mate, col)
     at_x = (me, 1 - col)
+
+    def place_of(k, c):
+        return ((k // hh) * 2 + c) * hh + lax.rem(k, hh)
+
+    spot = place_of(mine, core)
 
     def rcopy(src, dst, ss, rs, dev):
         return pltpu.make_async_remote_copy(
             src_ref=src, dst_ref=dst, send_sem=ss, recv_sem=rs,
             device_id=dev, device_id_type=pl.DeviceIdType.MESH)
 
+    def signal(sem, dev):
+        pl.semaphore_signal(sem, inc=1, device_id=dev, device_id_type=pl.DeviceIdType.MESH)
+
+    def at_peer(k):
+        return (2 * k + core, col)
+
+    near = min(4, half)
+    later = ((2, mine == 0), (1, (mine == 0) | (mine == 2)), (3, mine < 3))
+    earlier = ((0, mine > 0), (2, (mine == 1) | (mine > 2)), (1, mine > 2), (3, mine > 3))
+
+    def each(pairs, fn):
+        for k, cond in pairs:
+            pl.when(cond)(functools.partial(fn, k))
+
+    far_later = [(k, mine < k) for k in range(near, half)]
+    far_earlier = [(k, mine > k) for k in range(near, half - 1)]
+    n_earlier = jnp.where(mine == 1, 2, jnp.where(mine == 2, 1, mine))
+    n_far = jnp.where(mine < near, half - near, half - 1 - mine)
+
     barrier = pltpu.get_barrier_semaphore()
-    masks = [half >> k for k in range(1, half.bit_length())]
-    near = [(2 * (mine + m - 2 * m * lax.rem(mine // m, 2)) + core, col) for m in masks]
-    for dev in near + [at_mate, at_x]:
-        pl.semaphore_signal(barrier, inc=1, device_id=dev, device_id_type=pl.DeviceIdType.MESH)
+    signal(barrier, at_x)
+    signal(barrier, at_mate)
+    each(later, lambda k: signal(barrier, at_peer(k)))
+    each(far_later, lambda k: signal(barrier, at_peer(k)))
+
     small = []
+    step = q_w * btiles
+    loads = [pltpu.make_async_copy(
+        cnt_hbm.at[pl.ds(q * step, step), :], cnt_v.at[pl.ds(q * step, step), :], dsem.at[q])
+        for q in range(nq)]
     for k, (src, dst) in enumerate(((cm_hbm, cm_ref), (c_hbm, c_ref), (occ_hbm, occ_ref),
                                     (rm_hbm, rm_ref))):
         cp = pltpu.make_async_copy(src, dst, dsem.at[nq + 1 + k])
         cp.start()
         small.append(cp)
-    step = q_w * btiles
-    loads = []
-    for q in range(nq):
-        cp = pltpu.make_async_copy(
-            cnt_hbm.at[pl.ds(q * step, step), :], cnt_v.at[pl.ds(q * step, step), :], dsem.at[q])
+    for cp in loads:
         cp.start()
-        loads.append(cp)
     rload = pltpu.make_async_copy(r_hbm, r_v, dsem.at[nq])
     rload.start()
 
+    def enter():
+        pl.semaphore_wait(barrier, 2 + n_earlier)
+        slot = jnp.minimum(mine, near)
+        each(earlier, lambda k: signal(token.at[slot], at_peer(k)))
+        each(far_earlier, lambda k: signal(token.at[slot], at_peer(k)))
+
+    pl.when(mine >= 2)(enter)
     for cp in small:
         cp.wait()
 
@@ -110,14 +147,13 @@
     for at, val in ((d, hi), (d + 1, mid), (d + 2, lo)):
         own = jnp.where(li == at, val, own)
     own = jnp.where((li >= d + 3) & (li < d + 6), 1.0, own)
-    cg[0, me] = own.astype(jnp.bfloat16)
+    cg[0, spot] = own.astype(jnp.bfloat16)
 
     ident = eye(LANES)
 
     def encode(q):
         loads[q].wait()
-
-        def part(t):
+        for t in range(btiles):
             cells = []
             for u in range(q_w // tile):
                 x = cnt_v[pl.ds(q * step + u * tile * btiles + t, tile, stride=btiles), :]
@@ -125,53 +161,90 @@
                 on = jnp.broadcast_to(occ_ref[t:t + 1, k:k + 1], (tile, LANES)) != 0
                 cells.append(jnp.where(on, x, -1).astype(jnp.float32).astype(jnp.bfloat16))
             code = nt(ident, jnp.concatenate(cells, axis=0))
-            at = pl.ds(t * LANES, LANES)
-            enc[0, q, at, :] = code.astype(jnp.bfloat16)
-            slope_v[q, at, :], logc_v[q, at, :] = slope_terms(code)
-
-        for t in range(btiles):
-            part(t)
-
-    ecopies = [rcopy(enc.at[0, q], enc.at[1, q], e_s.at[q], e_r.at[q], at_x) for q in range(nq)]
+            slope, logc = slope_terms(code)
+            for r in range(LANES // w):
+                b = t * (LANES // w) + r
+                k = b // 2
+                at = pl.ds((((k // hh) * 2 + b % 2) * hh + k % hh) * w, w)
+                part = slice(r * w, (r + 1) * w)
+                enc[0, q, at, :] = code[part].astype(jnp.bfloat16)
+                slope_v[q, at, :] = slope[part]
+                logc_v[q, at, :] = logc[part]
+
+    ecopies = [rcopy(enc.at[0, q], enc.at[1, q], e_s, e_r.at[q], at_x) for q in range(nq)]
+    xcp = rcopy(cg.at[0, spot], cg.at[1, spot], gx_s, gx_r, at_x)
+
+    def to_near(which, waiting):
+        def one(k):
+            if waiting:
+                pl.semaphore_wait(token.at[k], 1)
+            if k == 2:
+                rcopy(cg.at[which, spot], cg.at[which, spot], g_s, w_r.at[which],
+                      at_peer(k)).start()
+            else:
+                direct(which, k)
+
+        each(later, one)
+
+    def direct(which, k):
+        rcopy(cg.at[which, spot], cg.at[which, spot], g_s, g_r.at[which, own_half],
+              at_peer(k)).start()
+
+    def to_earlier(which):
+        each(earlier, functools.partial(direct, which))
+        each(far_earlier, functools.partial(direct, which))
+
+    def to_far(which):
+        for k, cond in far_later:
+            pl.when(cond & (mine > 0))(functools.partial(direct, which, k))
+
+    def far_ready():
+        @pl.when(n_far > 0)
+        def _():
+            pl.semaphore_wait(token.at[near], n_far)
+
+    def relay(which):
+        @pl.when(mine == 2)
+        def _():
+            at = cg.at[which, place_of(0, core)]
+            rcopy(at, at, g_s, w_r.at[which], at_mate).wait_recv()
+            for k in range(near, half):
+                rcopy(at, at, g_s, g_r.at[which, 0], at_peer(k)).start()
+
+    def begin():
+        xcp.start()
+        to_earlier(0)
+
+    pl.when(mine >= 2)(begin)
     encode(0)
-    pl.semaphore_wait(barrier, len(masks) + 2)
+
+    @pl.when(mine < 2)
+    def _():
+        enter()
+        begin()
+
     ecopies[0].start()
-    xcp = rcopy(cg.at[0, me], cg.at[1, me], gx_s, gx_r, at_x)
-    xcp.start()
-    sends = [xcp]
-    cp = rcopy(cg.at[0, me], cg.at[0, me], gc_s.at[0, mine], gc_r.at[0, mine], at_mate)
-    cp.start()
-    sends.append(cp)
-
-    done = 1
-    for k in range(1, len(masks)):
-        pl.semaphore_signal(token.at[k], inc=1, device_id=near[k], device_id_type=pl.DeviceIdType.MESH)
-        if done < nq:
-            encode(done)
-        pl.semaphore_wait(token.at[k], 1)
-        if done < nq:
-            ecopies[done].start()
-            done += 1
-
-    for p in peers:
-        cp = rcopy(cg.at[0, me], cg.at[0, me], gz_s.at[0, p // 2], gz_r.at[0, mine], (p, col))
-        cp.start()
-        sends.append(cp)
-    for q in range(done, nq):
+    if nq > 1:
+        encode(1)
+    to_near(0, True)
+    if nq > 1:
+        ecopies[1].start()
+    if nq > 2:
+        encode(2)
+    pl.when(mine > 0)(far_ready)
+    to_far(0)
+    relay(0)
+    if nq > 2:
+        ecopies[2].start()
+    for q in range(3, nq):
         encode(q)
-        if q > done:
+        if q > 3:
             ecopies[q - 1].start()
-
     xcp.wait_recv()
-    for p in peers:
-        cp = rcopy(cg.at[1, me], cg.at[1, me], gz_s.at[1, p // 2], gz_r.at[1, mine], (p, col))
-        cp.start()
-        sends.append(cp)
-    cp = rcopy(cg.at[1, me], cg.at[1, me], gc_s.at[1, mine], gc_r.at[1, mine], at_mate)
-    cp.start()
-    sends.append(cp)
-
-    if done < nq:
+    to_earlier(1)
+    to_near(1, False)
+    to_far(1)
+    if nq > 3:
         ecopies[nq - 1].start()
 
     rload.wait()
@@ -186,76 +259,105 @@
         tail = jnp.where(si == at, val, tail)
     raug[pl.ds(first, dp - first), :] = tail.astype(jnp.bfloat16)
 
-    def forward(which):
-        for p in froms:
-            rcopy(cg.at[which, p], cg.at[which, p], gz_s.at[which, p // 2],
-                  gz_r.at[which, p // 2], at_mate).wait_recv()
-            cp = rcopy(cg.at[which, p], cg.at[which, p], gc_s.at[which, p // 2],
-                       gc_r.at[which, p // 2], at_mate)
-            cp.start()
-            sends.append(cp)
-
-    def mate_blocks(which):
-        for k in range(half):
-            at = 2 * k + 1 - core
-            rcopy(cg.at[which, at], cg.at[which, at], gc_s.at[which, k],
-                  gc_r.at[which, k], at_mate).wait_recv()
-
-    forward(0)
-    mate_blocks(0)
-
-    per = sub // w
-
-    def block(which, s):
-        return cg[which, pl.ds(s * per, per)].reshape(sub, dp)
-
-    for q in range(nq):
-        qs = pl.ds(q * q_w, q_w)
-
-        def cells(s):
-            at = pl.ds(s * sub, sub)
-            gap = nn(block(0, s), raug[:, qs])
-            code = enc[0, q, at, :].astype(jnp.float32)
-            res[at, qs] = cell(code, slope_v[q, at, :], logc_v[q, at, :], gap).astype(jnp.bfloat16)
-
-        repeat(nsub, cells)
-
-    def col_terms(s):
-        gcol[pl.ds(s * per, per)] = nt(res[pl.ds(s * sub, sub), :], raug[...]).reshape(per, w, dp)
-
-    repeat(nsub, col_terms)
-    for p in peers + [me]:
-        k = p // 2
-        cp = rcopy(gcol.at[2 * k + 1 - core], s1buf.at[k], a_s.at[k], a_r.at[k], at_mate)
-        cp.start()
-        sends.append(cp)
+    def arrived(which, h, blocks):
+        some = cg.at[which, pl.ds(0, blocks)]
+        rcopy(some, some, g_s, g_r.at[which, h], at_mate).wait_recv()
+
+    def to_mate(which, h):
+        part = cg.at[which, pl.ds((h * 2 + core) * hh, hh)]
+        return rcopy(part, part, m_s, m_r.at[which, h], at_mate)
+
+    def gathered(which, at):
+        h = halves[at]
+        if at:
+            arrived(which, h, hh)
+        else:
+            pl.when(mine == 2)(lambda: arrived(which, h, hh - 2))
+            pl.when(mine != 2)(lambda: arrived(which, h, hh - 1))
+        to_mate(which, h).start()
+
+    def block(which, first, count):
+        return cg[which, pl.ds(first, count)].reshape(count * w, dp)
+
+    def reduced(k):
+        return rcopy(s2src.at[k], s2buf.at[mine], b_s, b_r, at_peer(k))
+
+    def from_mate(h):
+        return rcopy(gcol.at[pl.ds((h * 2 + 1 - core) * hh, hh)], s1buf.at[pl.ds(h * hh, hh)],
+                     a_s, a_r.at[h], at_mate)
+
+    def half_terms(h):
+        for q in range(nq):
+            qs = pl.ds(q * q_w, q_w)
+
+            def cells(s):
+                at = pl.ds(pl.multiple_of(h * gcols + s * subg, subg), subg)
+                gap = nn(block(0, (h * gcols + s * subg) // w, subg // w), raug[:, qs])
+                code = enc[0, q, at, :].astype(jnp.float32)
+                res[at, qs] = cell(code, slope_v[q, at, :], logc_v[q, at, :], gap).astype(jnp.bfloat16)
+
+            repeat(nsubg, cells)
+
+        def terms(s):
+            at = pl.ds(pl.multiple_of(h * gcols + s * subg, subg), subg)
+            part = nt(res[at, :], raug[...]).reshape(subg // w, w, dp)
+            gcol[pl.ds((h * gcols + s * subg) // w, subg // w)] = part
+
+        repeat(nsubg, terms)
+
+    def spread(h, own):
+        from_mate(h).wait_recv()
+        for i in range(hh):
+            k = h * hh + i
+            total = gcol[(h * 2 + core) * hh + i] + s1buf[k]
+            s2src[k] = total.astype(s2src.dtype)
+            if own:
+                @pl.when(mine == k)
+                def _():
+                    blk[...] = total
+
+            if i and own:
+                pl.when(mine != k - 1)(lambda: reduced(k - 1).start())
+            elif i:
+                reduced(k - 1).start()
+
+    def spread_last(h, own):
+        k = h * hh + hh - 1
+        if own:
+            pl.when(mine != k)(lambda: reduced(k).start())
+        else:
+            reduced(k).start()
 
     ident_d = eye(dp)
 
     def transposed(which):
         def one(s):
-            cd[which, :, pl.ds(s * sub, sub)] = nt(ident_d, block(which, s)).astype(jnp.bfloat16)
+            part = block(which, s * (sub // w), sub // w)
+            cd[which, :, pl.ds(s * sub, sub)] = nt(ident_d, part).astype(jnp.bfloat16)
 
         repeat(nsub, one)
 
+    gathered(0, 0)
+    to_mate(0, own_half).wait_recv()
+    half_terms(own_half)
+    from_mate(own_half).start()
+    gathered(0, 1)
+    relay(1)
+    to_mate(0, 1 - own_half).wait_recv()
+    half_terms(1 - own_half)
+    pl.when(mine == 0)(far_ready)
+    from_mate(1 - own_half).start()
+    spread(own_half, True)
+    gathered(1, 0)
+    spread_last(own_half, True)
     transposed(0)
+    spread(1 - own_half, False)
+    gathered(1, 1)
+    spread_last(1 - own_half, False)
     rows_out[...] = nn(cd[0], res[...])[:d, :]
 
-    held = None
-    for p in peers + [me]:
-        rcopy(gcol.at[p], s1buf.at[p // 2], a_s.at[p // 2], a_r.at[p // 2], at_mate).wait_recv()
-        if p is me:
-            total = gcol[me] + s1buf[mine]
-        else:
-            s2src[p // 2] = (gcol[p] + s1buf[p // 2]).astype(s2src.dtype)
-        if held is not None:
-            held.start()
-            sends.append(held)
-        held = None if p is me else rcopy(
-            s2src.at[p // 2], s2buf.at[mine], b_s.at[p // 2], b_r.at[mine], (p, col))
-
-    forward(1)
-    mate_blocks(1)
+    to_mate(1, own_half).wait_recv()
+    to_mate(1, 1 - own_half).wait_recv()
     transposed(1)
     for q in range(nq):
         qs = pl.ds(q * q_w, q_w)
@@ -263,7 +365,7 @@
 
         def cells(s):
             at = pl.ds(s * sub, sub)
-            gap = nn(block(1, s), raug[:, qs])
+            gap = nn(block(1, s * (sub // w), sub // w), raug[:, qs])
             code = enc[1, q, at, :].astype(jnp.float32)
             slope, logc = slope_terms(code)
             res[at, qs] = cell(code, slope, logc, gap).astype(jnp.bfloat16)
@@ -271,12 +373,27 @@
         repeat(nsub, cells)
         rows_out[:, qs] = (rows_out[:, qs] + nn(cd[1], res[:, qs])[:d, :]) * scale_r
 
-    for p in froms:
-        rcopy(s2src.at[0], s2buf.at[p // 2], b_s.at[p // 2], b_r.at[p // 2], at_mate).wait_recv()
-        total = total + s2buf[p // 2].astype(jnp.float32)
+    got = s2buf.at[pl.ds(0, half - 1)]
+    summed = rcopy(got, got, b_s, b_r, at_mate)
+    summed.wait_recv()
+    total = blk[...]
+    for k in froms:
+        total = total + s2buf[k].astype(jnp.float32)
     cols_out[...] = (total * scale_c)[:, :d]
-    for cp in sends + ecopies:
-        cp.wait_send()
+
+    def sent(blocks):
+        some = gcol.at[pl.ds(0, blocks)]
+        rcopy(some, some, g_s, gx_r, at_mate).wait_send()
+
+    pl.when(mine == 0)(lambda: sent(near - 1))
+    pl.when(mine == 2)(lambda: sent(2 * half - 1 - near))
+    pl.when((mine != 0) & (mine != 2))(lambda: sent(half - 1))
+    xcp.wait_send()
+    rcopy(cg.at[0], cg.at[1], m_s, gx_r, at_mate).wait_send()
+    rcopy(enc.at[0], enc.at[1], e_s, gx_r, at_x).wait_send()
+    some = gcol.at[pl.ds(0, half)]
+    rcopy(some, some, a_s, gx_r, at_mate).wait_send()
+    summed.wait_send()
 
 
 def scratch_bytes(shapes):
@@ -328,9 +445,9 @@
         pltpu.VMEM((1, rows), jnp.int32),
         pltpu.VMEM((1, w), jnp.int32),
         dma(nq + 5),
-        dma(2, half), dma(2, half), dma(2, half), dma(2, half), dma(), dma(),
-        dma(nq), dma(nq), dma(half), dma(half), dma(half), dma(half),
-        pltpu.SemaphoreType.REGULAR((half.bit_length() - 1,)),
+        dma(), dma(nq), dma(), dma(), dma(), dma(2, 2), dma(2), dma(), dma(2, 2),
+        dma(), dma(2), dma(), dma(),
+        pltpu.SemaphoreType.REGULAR((5,)),
     ]
     limit = min(60 << 20, (6 << 20) + scratch_bytes(scratch[:18]) + 2 * d * rows * 4 + 24 * band * q_w)
     grad_rows, grad_cols = pl.pallas_call(

time: 23.2 us -> 21.5 us (0.927)
  Pallas kernels: 21.8 us -> 20.1 us
    pallas_call x1, Pallas kernels: 20.7 us -> 19 us  [body(): pl.pallas_call(functools.partial(kernel, cfg), out_shape=(jax.ShapeDtypeS...]
where the time goes in v1:
time: 21.5 us; the launch traced here: 21.3 us
  Pallas kernels  20.1 us (93%)
  between operations  1.29 us (6%)
    pallas_call x1, Pallas kernels, body(): pl.pallas_call(functools.partial(kernel, cfg), out_shape=(jax.ShapeDtypeS...  19 us
    pallas_call x1, Pallas kernels, body(): pl.pallas_call(place, out_shape=(jax.ShapeDtypeStruct((d, rows), f32), ja...  1.06 us

profile of v1, /device:TPU:0, one launch (start us, length us, event | category | flops | bytes accessed | tf_op | source)
XLA Modules:
  0.0 21.3 jit_solution(10466276483490892687)
XLA Ops:
  1.3 19.0 %shard_map.86 = (f32[300,1024]{1,0:T(8,128)S(1)}, f32[16,300]{1,0:T(8,128)S(1)}) custom-call(bf16[300,1024]{1,0:T(8,128)(2,1)} %r_hbm.1, bf16[16,300]{1,0:T(8,128)(2,1)} %bitcast.12, s32[2048,128]{1,0:T(8,128)} %bitcast.11, s32[2,8]{1,0:T(2,128)} %bitcast.14, s32[1,1024]{1,0:T(1,128)} %bitcast.13, s32[1,16]{1,0:T(1,128)} %cm_hbm.1, f32[1]{0:T(128)S(6)} %copy.9.lt_ref), custom_call_target="tpu_custom_call" | custom-call | tf_op jit(solution)/shard_map/pallas_call | solution.py:453
  20.3 1.1 %shard_map.87 = (f32[300,1024]{1,0:T(8,128)}, f32[16,300]{1,0:T(8,128)}) custom-call(f32[300,1024]{1,0:T(8,128)S(1)} %get-tuple-element.6.rows_in, f32[16,300]{1,0:T(8,128)S(1)} %get-tuple-element.7.cols_in), custom_call_target="tpu_custom_call" | custom-call | tf_op jit(solution)/shard_map/pallas_call | solution.py:472

commit v2 on v1

--- a/solution.py
+++ b/solution.py
@@ -52,10 +52,11 @@
 def kernel(cfg, r_hbm, c_hbm, cnt_hbm, occ_hbm, rm_hbm, cm_hbm, lt_ref,
            rows_out, cols_out,
            r_v, cnt_v, raug, blk, cg, cd, enc, slope_v, logc_v, res, gcol, s1buf, s2src, s2buf,
-           c_ref, occ_ref, rm_ref, cm_ref, dsem, e_s, e_r, gx_s, gx_r, g_s, g_r, w_r, m_s, m_r,
-           a_s, a_r, b_s, b_r, token):
+           c_ref, occ_ref, rm_ref, cm_ref, dsem, e_s, e_r, gx_s, gx_r, g_s, g_r, w_s, w_r, m_s, m_r,
+           a_s, a_r, b_s, b_r, token, x_token, c_s, c_r, s0src, s0buf, res0):
     n, d, dp, w, band, rows, tile, q_w, scale_r, scale_c = cfg
     half = n // 2
+    dq = -(-d // 16) * 16
     hh = half // 2
     nq = rows // q_w
     btiles = band // LANES
@@ -91,9 +92,11 @@
     def at_peer(k):
         return (2 * k + core, col)
 
-    near = min(4, half)
-    later = ((2, mine == 0), (1, (mine == 0) | (mine == 2)), (3, mine < 3))
-    earlier = ((0, mine > 0), (2, (mine == 1) | (mine > 2)), (1, mine > 2), (3, mine > 3))
+    near = hh
+    later = [(2, mine == 0), (1, (mine == 0) | (mine == 2))]
+    later += [(k, mine < k) for k in range(3, near)]
+    earlier = [(0, mine > 0), (2, (mine == 1) | (mine > 2)), (1, mine > 2)]
+    earlier += [(k, mine > k) for k in range(3, near)]
 
     def each(pairs, fn):
         for k, cond in pairs:
@@ -105,7 +108,7 @@
     n_far = jnp.where(mine < near, half - near, half - 1 - mine)
 
     barrier = pltpu.get_barrier_semaphore()
-    signal(barrier, at_x)
+    pl.when(col == 0)(lambda: signal(barrier, at_x))
     signal(barrier, at_mate)
     each(later, lambda k: signal(barrier, at_peer(k)))
     each(far_later, lambda k: signal(barrier, at_peer(k)))
@@ -123,15 +126,13 @@
     for cp in loads:
         cp.start()
     rload = pltpu.make_async_copy(r_hbm, r_v, dsem.at[nq])
-    rload.start()
-
-    def enter():
-        pl.semaphore_wait(barrier, 2 + n_earlier)
-        slot = jnp.minimum(mine, near)
-        each(earlier, lambda k: signal(token.at[slot], at_peer(k)))
-        each(far_earlier, lambda k: signal(token.at[slot], at_peer(k)))
-
-    pl.when(mine >= 2)(enter)
+
+    pl.semaphore_wait(barrier, 1 + col + n_earlier)
+    slot = jnp.minimum(mine, near)
+    pl.when(col == 1)(lambda: signal(x_token, at_x))
+    each(earlier, lambda k: signal(token.at[slot], at_peer(k)))
+    each(far_earlier, lambda k: signal(token.at[slot], at_peer(k)))
+
     for cp in small:
         cp.wait()
 
@@ -166,10 +167,14 @@
                 b = t * (LANES // w) + r
                 k = b // 2
                 at = pl.ds((((k // hh) * 2 + b % 2) * hh + k % hh) * w, w)
-                part = slice(r * w, (r + 1) * w)
-                enc[0, q, at, :] = code[part].astype(jnp.bfloat16)
-                slope_v[q, at, :] = slope[part]
-                logc_v[q, at, :] = logc[part]
+                some = slice(r * w, (r + 1) * w)
+                enc[0, q, at, :] = code[some].astype(jnp.bfloat16)
+                slope_v[q, at, :] = slope[some]
+                logc_v[q, at, :] = logc[some]
+
+    def x_start(q, part):
+        at = pl.ds(pl.multiple_of(part * gcols, gcols), gcols)
+        rcopy(enc.at[0, q, at], enc.at[1, q, at], e_s, e_r.at[q], at_x).start()
 
     ecopies = [rcopy(enc.at[0, q], enc.at[1, q], e_s, e_r.at[q], at_x) for q in range(nq)]
     xcp = rcopy(cg.at[0, spot], cg.at[1, spot], gx_s, gx_r, at_x)
@@ -207,45 +212,45 @@
         @pl.when(mine == 2)
         def _():
             at = cg.at[which, place_of(0, core)]
-            rcopy(at, at, g_s, w_r.at[which], at_mate).wait_recv()
+            rcopy(at, at, w_s, w_r.at[which], at_mate).wait_recv()
             for k in range(near, half):
-                rcopy(at, at, g_s, g_r.at[which, 0], at_peer(k)).start()
-
-    def begin():
-        xcp.start()
-        to_earlier(0)
-
-    pl.when(mine >= 2)(begin)
+                if which:
+                    rcopy(at, at, w_s, g_r.at[which, 0], at_peer(k)).start()
+                else:
+                    for c in range(2):
+                        rcopy(at, at, w_s, w_r.at[which], (2 * k + c, col)).start()
+
+    to_earlier(0)
     encode(0)
 
-    @pl.when(mine < 2)
+    @pl.when(mine >= near)
     def _():
-        enter()
-        begin()
-
-    ecopies[0].start()
-    if nq > 1:
+        far_ready()
+        to_far(0)
+
+    pl.when(col == 0)(lambda: pl.semaphore_wait(x_token, 1))
+    xcp.start()
+    x_start(0, 0)
+    x_start(0, 1)
+    if nq > 2:
         encode(1)
     to_near(0, True)
-    if nq > 1:
-        ecopies[1].start()
-    if nq > 2:
-        encode(2)
-    pl.when(mine > 0)(far_ready)
-    to_far(0)
+
+    @pl.when((mine > 0) & (mine < near))
+    def _():
+        far_ready()
+        to_far(0)
+
     relay(0)
-    if nq > 2:
-        ecopies[2].start()
-    for q in range(3, nq):
+    rload.start()
+    for q in range(2, nq):
+        x_start(q - 1, 0)
+        x_start(q - 1, 1)
         encode(q)
-        if q > 3:
-            ecopies[q - 1].start()
     xcp.wait_recv()
     to_earlier(1)
     to_near(1, False)
     to_far(1)
-    if nq > 3:
-        ecopies[nq - 1].start()
 
     rload.wait()
     raug[pl.ds(0, d), :] = r_v[...]
@@ -263,18 +268,54 @@
         some = cg.at[which, pl.ds(0, blocks)]
         rcopy(some, some, g_s, g_r.at[which, h], at_mate).wait_recv()
 
-    def to_mate(which, h):
-        part = cg.at[which, pl.ds((h * 2 + core) * hh, hh)]
+    def to_mate(which, h, skip):
+        part = cg.at[which, pl.ds((h * 2 + core) * hh + skip, hh - skip)]
         return rcopy(part, part, m_s, m_r.at[which, h], at_mate)
 
     def gathered(which, at):
         h = halves[at]
-        if at:
-            arrived(which, h, hh)
+
+        def took(blocks, skip):
+            arrived(which, h, blocks)
+            to_mate(which, h, skip).start()
+
+        if at and which:
+            took(hh, 0)
+        elif at:
+            pl.when(mine < hh)(lambda: took(hh, 0))
+            pl.when(mine >= hh)(lambda: took(hh - 1, 1))
         else:
-            pl.when(mine == 2)(lambda: arrived(which, h, hh - 2))
-            pl.when(mine != 2)(lambda: arrived(which, h, hh - 1))
-        to_mate(which, h).start()
+            pl.when(mine == 2)(lambda: took(hh - 2, 0))
+            pl.when(mine != 2)(lambda: took(hh - 1, 0))
+
+    def from_mate_blocks(which, at):
+        h = halves[at]
+        if at and not which:
+            pl.when(mine < hh)(lambda: to_mate(which, h, 0).wait_recv())
+            pl.when(mine >= hh)(lambda: to_mate(which, h, 1).wait_recv())
+        else:
+            to_mate(which, h, 0).wait_recv()
+
+    def first_chip():
+        two = cg.at[0, pl.ds(0, 2)]
+        rcopy(two, two, w_s, w_r.at[0], at_mate).wait_recv()
+        ends = (pl.ds(0, w), pl.ds(hh * w, w))
+
+        def both(fn):
+            return jnp.concatenate([fn(at) for at in ends], axis=0)
+
+        blocks = jnp.concatenate([cg[0, 0], cg[0, hh]], axis=0)
+        for q in range(nq):
+            qs = pl.ds(q * q_w, q_w)
+            gap = nn(blocks, raug[:, qs])
+            code = both(lambda at: enc[0, q, at, :]).astype(jnp.float32)
+            slope = both(lambda at: slope_v[q, at, :])
+            logc = both(lambda at: logc_v[q, at, :])
+            res0[:, qs] = cell(code, slope, logc, gap).astype(jnp.bfloat16)
+        s0src[...] = nt(res0[...], raug[...]).reshape(2, w, dp).astype(jnp.bfloat16)
+        spare = (mine - hh) * 2 + core
+        for c in range(2):
+            rcopy(s0src.at[c], s0buf.at[spare], c_s, c_r, (c, col)).start()
 
     def block(which, first, count):
         return cg[which, pl.ds(first, count)].reshape(count * w, dp)
@@ -294,7 +335,10 @@
                 at = pl.ds(pl.multiple_of(h * gcols + s * subg, subg), subg)
                 gap = nn(block(0, (h * gcols + s * subg) // w, subg // w), raug[:, qs])
                 code = enc[0, q, at, :].astype(jnp.float32)
-                res[at, qs] = cell(code, slope_v[q, at, :], logc_v[q, at, :], gap).astype(jnp.bfloat16)
+                got = cell(code, slope_v[q, at, :], logc_v[q, at, :], gap).astype(jnp.bfloat16)
+                res[at, qs] = got
+                if q == nq - 1:
+                    enc[0, q, at, :] = got
 
             repeat(nsubg, cells)
 
@@ -318,6 +362,8 @@
 
             if i and own:
                 pl.when(mine != k - 1)(lambda: reduced(k - 1).start())
+            elif i == 1:
+                pl.when(mine < hh)(lambda: reduced(k - 1).start())
             elif i:
                 reduced(k - 1).start()
 
@@ -330,70 +376,123 @@
 
     ident_d = eye(dp)
 
-    def transposed(which):
+    def transposed(which, h):
         def one(s):
-            part = block(which, s * (sub // w), sub // w)
-            cd[which, :, pl.ds(s * sub, sub)] = nt(ident_d, part).astype(jnp.bfloat16)
-
-        repeat(nsub, one)
+            part = block(which, (h * gcols + s * subg) // w, subg // w)
+            at = pl.ds(pl.multiple_of(h * gcols + s * subg, subg), subg)
+            cd[which, :, at] = nt(ident_d, part).astype(jnp.bfloat16)
+
+        repeat(nsubg, one)
+
+    def other_cells(q, h):
+        qs = pl.ds(q * q_w, q_w)
+
+        def cells(s):
+            at = pl.ds(pl.multiple_of(h * gcols + s * subg, subg), subg)
+            gap = nn(block(1, (h * gcols + s * subg) // w, subg // w), raug[:, qs])
+            code = enc[1, q, at, :].astype(jnp.float32)
+            slope, logc = slope_terms(code)
+            enc[1, q, at, :] = cell(code, slope, logc, gap).astype(jnp.bfloat16)
+
+        repeat(nsubg, cells)
+
+    def other_rows(q):
+        qs = pl.ds(q * q_w, q_w)
+        more = nn(cd[1, :dq, :], enc[1, q])[:d, :]
+        rows_out[:, qs] = (rows_out[:, qs] + more) * scale_r
 
     gathered(0, 0)
-    to_mate(0, own_half).wait_recv()
+    from_mate_blocks(0, 0)
     half_terms(own_half)
     from_mate(own_half).start()
+    x_start(nq - 1, own_half)
+    pl.when(mine >= hh)(first_chip)
     gathered(0, 1)
     relay(1)
-    to_mate(0, 1 - own_half).wait_recv()
+    from_mate_blocks(0, 1)
     half_terms(1 - own_half)
     pl.when(mine == 0)(far_ready)
     from_mate(1 - own_half).start()
+    x_start(nq - 1, 1 - own_half)
     spread(own_half, True)
     gathered(1, 0)
     spread_last(own_half, True)
-    transposed(0)
+    transposed(0, 0)
+    transposed(0, 1)
     spread(1 - own_half, False)
+    spread_last(1 - own_half, False)
+    rows_out[...] = nn(cd[0, :dq, :], res[...])[:d, :]
+
+    from_mate_blocks(1, 0)
+    transposed(1, own_half)
+    sooner = nq // 2
+    for q in range(sooner):
+        ecopies[q].wait_recv()
+        other_cells(q, own_half)
     gathered(1, 1)
-    spread_last(1 - own_half, False)
-    rows_out[...] = nn(cd[0], res[...])[:d, :]
-
-    to_mate(1, own_half).wait_recv()
-    to_mate(1, 1 - own_half).wait_recv()
-    transposed(1)
-    for q in range(nq):
-        qs = pl.ds(q * q_w, q_w)
+    from_mate_blocks(1, 1)
+    transposed(1, 1 - own_half)
+    for q in range(sooner):
+        other_cells(q, 1 - own_half)
+        other_rows(q)
+    for q in range(sooner, nq):
         ecopies[q].wait_recv()
-
-        def cells(s):
-            at = pl.ds(s * sub, sub)
-            gap = nn(block(1, s * (sub // w), sub // w), raug[:, qs])
-            code = enc[1, q, at, :].astype(jnp.float32)
-            slope, logc = slope_terms(code)
-            res[at, qs] = cell(code, slope, logc, gap).astype(jnp.bfloat16)
-
-        repeat(nsub, cells)
-        rows_out[:, qs] = (rows_out[:, qs] + nn(cd[1], res[:, qs])[:d, :]) * scale_r
-
-    got = s2buf.at[pl.ds(0, half - 1)]
-    summed = rcopy(got, got, b_s, b_r, at_mate)
-    summed.wait_recv()
-    total = blk[...]
-    for k in froms:
-        total = total + s2buf[k].astype(jnp.float32)
-    cols_out[...] = (total * scale_c)[:, :d]
+        if q < nq - 1:
+            other_cells(q, 0)
+            other_cells(q, 1)
+        other_rows(q)
+
+    def summed(blocks):
+        got = s2buf.at[pl.ds(0, blocks)]
+        return rcopy(got, got, b_s, b_r, at_mate)
+
+    @pl.when(mine == 0)
+    def _():
+        summed(hh - 1).wait_recv()
+        total = blk[...]
+        for k in range(1, hh):
+            total = total + s2buf[k].astype(jnp.float32)
+        rcopy(s0buf, s0buf, c_s, c_r, at_mate).wait_recv()
+        for k in range(half):
+            total = total + s0buf[k].astype(jnp.float32)
+        cols_out[...] = (total * scale_c)[:, :d]
+
+    @pl.when(mine != 0)
+    def _():
+        summed(half - 1).wait_recv()
+        total = blk[...]
+        for k in froms:
+            total = total + s2buf[k].astype(jnp.float32)
+        cols_out[...] = (total * scale_c)[:, :d]
 
     def sent(blocks):
         some = gcol.at[pl.ds(0, blocks)]
         rcopy(some, some, g_s, gx_r, at_mate).wait_send()
 
     pl.when(mine == 0)(lambda: sent(near - 1))
-    pl.when(mine == 2)(lambda: sent(2 * half - 1 - near))
-    pl.when((mine != 0) & (mine != 2))(lambda: sent(half - 1))
+    pl.when(mine != 0)(lambda: sent(half - 1))
+
+    @pl.when(mine == 2)
+    def _():
+        some = gcol.at[pl.ds(0, 3 * (half - near) // 2)]
+        rcopy(some, some, w_s, gx_r, at_mate).wait_send()
+
     xcp.wait_send()
-    rcopy(cg.at[0], cg.at[1], m_s, gx_r, at_mate).wait_send()
+    def told(blocks):
+        some = cg.at[0, pl.ds(0, blocks)]
+        rcopy(some, some, m_s, gx_r, at_mate).wait_send()
+
+    pl.when(mine < hh)(lambda: told(n))
+    pl.when(mine >= hh)(lambda: told(n - 1))
     rcopy(enc.at[0], enc.at[1], e_s, gx_r, at_x).wait_send()
     some = gcol.at[pl.ds(0, half)]
     rcopy(some, some, a_s, gx_r, at_mate).wait_send()
-    summed.wait_send()
+    pl.when(mine < hh)(lambda: summed(half - 1).wait_send())
+
+    @pl.when(mine >= hh)
+    def _():
+        summed(half - 2).wait_send()
+        rcopy(s0src, s0src, c_s, c_r, at_mate).wait_send()
 
 
 def scratch_bytes(shapes):
@@ -445,11 +544,16 @@
         pltpu.VMEM((1, rows), jnp.int32),
         pltpu.VMEM((1, w), jnp.int32),
         dma(nq + 5),
-        dma(), dma(nq), dma(), dma(), dma(), dma(2, 2), dma(2), dma(), dma(2, 2),
+        dma(), dma(nq), dma(), dma(), dma(), dma(2, 2), dma(), dma(2), dma(), dma(2, 2),
         dma(), dma(2), dma(), dma(),
-        pltpu.SemaphoreType.REGULAR((5,)),
+        pltpu.SemaphoreType.REGULAR((half // 2 + 1,)),
+        pltpu.SemaphoreType.REGULAR,
+        dma(), dma(),
+        pltpu.VMEM((2, w, dp), bf),
+        pltpu.VMEM((half, w, dp), bf),
+        pltpu.VMEM((2 * w, rows), bf),
     ]
-    limit = min(60 << 20, (6 << 20) + scratch_bytes(scratch[:18]) + 2 * d * rows * 4 + 24 * band * q_w)
+    limit = min(60 << 20, (6 << 20) + scratch_bytes(scratch[:18]) + 2 * d * rows * 4 + 28 * band * q_w)
     grad_rows, grad_cols = pl.pallas_call(
         functools.partial(kernel, cfg),
         out_shape=(jax.ShapeDtypeStruct((d, rows), f32), jax.ShapeDtypeStruct((w, d), f32)),

time: 21.5 us -> 20 us (0.930)
  Pallas kernels: 20.1 us -> 18.4 us
    pallas_call x1, Pallas kernels: 19 us -> 17.3 us  [body(): pl.pallas_call(functools.partial(kernel, cfg), out_shape=(jax.ShapeDtypeS...]
where the time goes in v2:
time: 20 us; the launch traced here: 19.7 us
  Pallas kernels  18.4 us (92%)
  between operations  1.29 us (6%)
    pallas_call x1, Pallas kernels, body(): pl.pallas_call(functools.partial(kernel, cfg), out_shape=(jax.ShapeDtypeS...  17.3 us
    pallas_call x1, Pallas kernels, body(): pl.pallas_call(place, out_shape=(jax.ShapeDtypeStruct((d, rows), f32), ja...  1.06 us

profile of v2, /device:TPU:0, one launch (start us, length us, event | category | flops | bytes accessed | tf_op | source)
XLA Modules:
  0.0 19.7 jit_solution(12462201430900287360)
XLA Ops:
  1.3 17.3 %shard_map.86 = (f32[300,1024]{1,0:T(8,128)S(1)}, f32[16,300]{1,0:T(8,128)S(1)}) custom-call(bf16[300,1024]{1,0:T(8,128)(2,1)} %r_hbm.1, bf16[16,300]{1,0:T(8,128)(2,1)} %bitcast.12, s32[2048,128]{1,0:T(8,128)} %bitcast.11, s32[2,8]{1,0:T(2,128)} %bitcast.14, s32[1,1024]{1,0:T(1,128)} %bitcast.13, s32[1,16]{1,0:T(1,128)} %cm_hbm.1, f32[1]{0:T(128)S(6)} %copy.9.lt_ref), custom_call_target="tpu_custom_call" | custom-call | tf_op jit(solution)/shard_map/pallas_call | solution.py:557
  18.6 1.1 %shard_map.87 = (f32[300,1024]{1,0:T(8,128)}, f32[16,300]{1,0:T(8,128)}) custom-call(f32[300,1024]{1,0:T(8,128)S(1)} %get-tuple-element.6.rows_in, f32[16,300]{1,0:T(8,128)S(1)} %get-tuple-element.7.cols_in), custom_call_target="tpu_custom_call" | custom-call | tf_op jit(solution)/shard_map/pallas_call | solution.py:576

commit v3 on v2

--- a/solution.py
+++ b/solution.py
@@ -118,12 +118,13 @@
     loads = [pltpu.make_async_copy(
         cnt_hbm.at[pl.ds(q * step, step), :], cnt_v.at[pl.ds(q * step, step), :], dsem.at[q])
         for q in range(nq)]
+    loads[0].start()
     for k, (src, dst) in enumerate(((cm_hbm, cm_ref), (c_hbm, c_ref), (occ_hbm, occ_ref),
                                     (rm_hbm, rm_ref))):
         cp = pltpu.make_async_copy(src, dst, dsem.at[nq + 1 + k])
         cp.start()
         small.append(cp)
-    for cp in loads:
+    for cp in loads[1:]:
         cp.start()
     rload = pltpu.make_async_copy(r_hbm, r_v, dsem.at[nq])
 
@@ -152,7 +153,7 @@
 
     ident = eye(LANES)
 
-    def encode(q):
+    def codes(q):
         loads[q].wait()
         for t in range(btiles):
             cells = []
@@ -161,20 +162,31 @@
                 k = q * (q_w // tile) + u
                 on = jnp.broadcast_to(occ_ref[t:t + 1, k:k + 1], (tile, LANES)) != 0
                 cells.append(jnp.where(on, x, -1).astype(jnp.float32).astype(jnp.bfloat16))
-            code = nt(ident, jnp.concatenate(cells, axis=0))
-            slope, logc = slope_terms(code)
+            code = nt(ident, jnp.concatenate(cells, axis=0)).astype(jnp.bfloat16)
             for r in range(LANES // w):
                 b = t * (LANES // w) + r
                 k = b // 2
                 at = pl.ds((((k // hh) * 2 + b % 2) * hh + k % hh) * w, w)
-                some = slice(r * w, (r + 1) * w)
-                enc[0, q, at, :] = code[some].astype(jnp.bfloat16)
-                slope_v[q, at, :] = slope[some]
-                logc_v[q, at, :] = logc[some]
+                enc[0, q, at, :] = code[r * w:(r + 1) * w]
+
+    def slopes(q):
+        def one(s):
+            at = pl.ds(s * sub, sub)
+            slope_v[q, at, :], logc_v[q, at, :] = slope_terms(enc[0, q, at, :].astype(jnp.float32))
+
+        repeat(nsub, one)
+
+    def encode(q):
+        codes(q)
+        slopes(q)
 
     def x_start(q, part):
         at = pl.ds(pl.multiple_of(part * gcols, gcols), gcols)
         rcopy(enc.at[0, q, at], enc.at[1, q, at], e_s, e_r.at[q], at_x).start()
+
+    def x_starts(q):
+        x_start(q, 0)
+        x_start(q, 1)
 
     ecopies = [rcopy(enc.at[0, q], enc.at[1, q], e_s, e_r.at[q], at_x) for q in range(nq)]
     xcp = rcopy(cg.at[0, spot], cg.at[1, spot], gx_s, gx_r, at_x)
@@ -221,48 +233,45 @@
                         rcopy(at, at, w_s, w_r.at[which], (2 * k + c, col)).start()
 
     to_earlier(0)
-    encode(0)
+    codes(0)
+
+    def cross():
+        pl.when(col == 0)(lambda: pl.semaphore_wait(x_token, 1))
+        xcp.start()
+        x_starts(0)
+
+    first = (col == 1) | (mine < near)
+    pl.when(first)(cross)
 
     @pl.when(mine >= near)
     def _():
         far_ready()
         to_far(0)
 
-    pl.when(col == 0)(lambda: pl.semaphore_wait(x_token, 1))
-    xcp.start()
-    x_start(0, 0)
-    x_start(0, 1)
+    pl.when(jnp.logical_not(first))(cross)
+    slopes(0)
     if nq > 2:
         encode(1)
     to_near(0, True)
-
-    @pl.when((mine > 0) & (mine < near))
-    def _():
-        far_ready()
-        to_far(0)
-
+    pl.when((mine > 0) & (mine < near))(far_ready)
     relay(0)
+    pl.when(mine < near)(lambda: to_far(0))
     rload.start()
     for q in range(2, nq):
-        x_start(q - 1, 0)
-        x_start(q - 1, 1)
+        x_starts(q - 1)
         encode(q)
-    xcp.wait_recv()
-    to_earlier(1)
-    to_near(1, False)
-    to_far(1)
 
     rload.wait()
     raug[pl.ds(0, d), :] = r_v[...]
-    first = (d // 16) * 16
+    base = (d // 16) * 16
     row_term = jnp.log(rm_ref[...].astype(jnp.float32)) - lt_ref[0]
     hi, mid, lo = split3(row_term)
-    tail = raug[pl.ds(first, dp - first), :].astype(jnp.float32)
-    si = lax.broadcasted_iota(jnp.int32, (dp - first, rows), 0) + first
+    tail = raug[pl.ds(base, dp - base), :].astype(jnp.float32)
+    si = lax.broadcasted_iota(jnp.int32, (dp - base, rows), 0) + base
     tail = jnp.where(si < d, tail, jnp.where(si < d + 3, 1.0, 0.0))
     for at, val in ((d + 3, hi), (d + 4, mid), (d + 5, lo)):
         tail = jnp.where(si == at, val, tail)
-    raug[pl.ds(first, dp - first), :] = tail.astype(jnp.bfloat16)
+    raug[pl.ds(base, dp - base), :] = tail.astype(jnp.bfloat16)
 
     def arrived(which, h, blocks):
         some = cg.at[which, pl.ds(0, blocks)]
@@ -401,12 +410,16 @@
         more = nn(cd[1, :dq, :], enc[1, q])[:d, :]
         rows_out[:, qs] = (rows_out[:, qs] + more) * scale_r
 
+    xcp.wait_recv()
+    to_earlier(1)
+    to_near(1, False)
     gathered(0, 0)
     from_mate_blocks(0, 0)
     half_terms(own_half)
     from_mate(own_half).start()
     x_start(nq - 1, own_half)
     pl.when(mine >= hh)(first_chip)
+    to_far(1)
     gathered(0, 1)
     relay(1)
     from_mate_blocks(0, 1)
@@ -415,12 +428,12 @@
     from_mate(1 - own_half).start()
     x_start(nq - 1, 1 - own_half)
     spread(own_half, True)
+    transposed(0, 0)
+    spread_last(own_half, True)
+    spread(1 - own_half, False)
+    transposed(0, 1)
+    spread_last(1 - own_half, False)
     gathered(1, 0)
-    spread_last(own_half, True)
-    transposed(0, 0)
-    transposed(0, 1)
-    spread(1 - own_half, False)
-    spread_last(1 - own_half, False)
     rows_out[...] = nn(cd[0, :dq, :], res[...])[:d, :]
 
     from_mate_blocks(1, 0)

time: 20 us -> 19.7 us (0.985)
  no operation moved by 1% of the time
where the time goes in v3:
time: 19.7 us; the launch traced here: 19.5 us
  Pallas kernels  18.2 us (92%)
  between operations  1.29 us (7%)
    pallas_call x1, Pallas kernels, body(): pl.pallas_call(functools.partial(kernel, cfg), out_shape=(jax.ShapeDtypeS...  17.2 us
    pallas_call x1, Pallas kernels, body(): pl.pallas_call(place, out_shape=(jax.ShapeDtypeStruct((d, rows), f32), ja...  1.06 us

profile of v3, /device:TPU:0, one launch (start us, length us, event | category | flops | bytes accessed | tf_op | source)
XLA Modules:
  0.0 19.5 jit_solution(5667531483837235011)
XLA Ops:
  1.3 17.2 %shard_map.86 = (f32[300,1024]{1,0:T(8,128)S(1)}, f32[16,300]{1,0:T(8,128)S(1)}) custom-call(bf16[300,1024]{1,0:T(8,128)(2,1)} %r_hbm.1, bf16[16,300]{1,0:T(8,128)(2,1)} %bitcast.12, s32[2048,128]{1,0:T(8,128)} %bitcast.11, s32[2,8]{1,0:T(2,128)} %bitcast.14, s32[1,1024]{1,0:T(1,128)} %bitcast.13, s32[1,16]{1,0:T(1,128)} %cm_hbm.1, f32[1]{0:T(128)S(6)} %copy.9.lt_ref), custom_call_target="tpu_custom_call" | custom-call | tf_op jit(solution)/shard_map/pallas_call | solution.py:570
  18.5 1.1 %shard_map.87 = (f32[300,1024]{1,0:T(8,128)}, f32[16,300]{1,0:T(8,128)}) custom-call(f32[300,1024]{1,0:T(8,128)S(1)} %get-tuple-element.6.rows_in, f32[16,300]{1,0:T(8,128)S(1)} %get-tuple-element.7.cols_in), custom_call_target="tpu_custom_call" | custom-call | tf_op jit(solution)/shard_map/pallas_call | solution.py:589

commit v4 on v3

--- a/solution.py
+++ b/solution.py
@@ -50,8 +50,8 @@
 
 
 def kernel(cfg, r_hbm, c_hbm, cnt_hbm, occ_hbm, rm_hbm, cm_hbm, lt_ref,
-           rows_out, cols_out,
-           r_v, cnt_v, raug, blk, cg, cd, enc, slope_v, logc_v, res, gcol, s1buf, s2src, s2buf,
+           rows_out, cols_out, cd1, last,
+           r_v, cnt_v, raug, blk, cg, cd0, enc, slope_v, logc_v, res, gcol, s1buf, s2src, s2buf,
            c_ref, occ_ref, rm_ref, cm_ref, dsem, e_s, e_r, gx_s, gx_r, g_s, g_r, w_s, w_r, m_s, m_r,
            a_s, a_r, b_s, b_r, token, x_token, c_s, c_r, s0src, s0buf, res0):
     n, d, dp, w, band, rows, tile, q_w, scale_r, scale_c = cfg
@@ -389,7 +389,7 @@
         def one(s):
             part = block(which, (h * gcols + s * subg) // w, subg // w)
             at = pl.ds(pl.multiple_of(h * gcols + s * subg, subg), subg)
-            cd[which, :, at] = nt(ident_d, part).astype(jnp.bfloat16)
+            (cd1 if which else cd0)[:, at] = nt(ident_d, part)[:dq, :].astype(jnp.bfloat16)
 
         repeat(nsubg, one)
 
@@ -407,7 +407,7 @@
 
     def other_rows(q):
         qs = pl.ds(q * q_w, q_w)
-        more = nn(cd[1, :dq, :], enc[1, q])[:d, :]
+        more = nn(cd1[...], enc[1, q])[:d, :]
         rows_out[:, qs] = (rows_out[:, qs] + more) * scale_r
 
     xcp.wait_recv()
@@ -434,15 +434,15 @@
     transposed(0, 1)
     spread_last(1 - own_half, False)
     gathered(1, 0)
-    rows_out[...] = nn(cd[0, :dq, :], res[...])[:d, :]
-
+    rows_out[...] = nn(cd0[...], res[...])[:d, :]
+
+    gathered(1, 1)
     from_mate_blocks(1, 0)
     transposed(1, own_half)
     sooner = nq // 2
     for q in range(sooner):
         ecopies[q].wait_recv()
         other_cells(q, own_half)
-    gathered(1, 1)
     from_mate_blocks(1, 1)
     transposed(1, 1 - own_half)
     for q in range(sooner):
@@ -453,7 +453,9 @@
         if q < nq - 1:
             other_cells(q, 0)
             other_cells(q, 1)
-        other_rows(q)
+            other_rows(q)
+        else:
+            last[...] = enc[1, q]
 
     def summed(blocks):
         got = s2buf.at[pl.ds(0, blocks)]
@@ -512,11 +514,17 @@
     return sum(math.prod(s.shape) * jnp.dtype(s.dtype).itemsize for s in shapes)
 
 
-def place(rows_in, cols_in, rows_out, cols_out, sem):
-    copies = [pltpu.make_async_copy(rows_in, rows_out, sem.at[0]),
-              pltpu.make_async_copy(cols_in, cols_out, sem.at[1])]
-    for cp in copies:
-        cp.start()
+def place(scale_r, rows_in, cols_in, cd1, last, rows_out, cols_out, end, sem):
+    d, rows = rows_in.shape
+    done = rows - last.shape[1]
+    copies = [pltpu.make_async_copy(cols_in, cols_out, sem.at[0]),
+              pltpu.make_async_copy(rows_in.at[:, pl.ds(0, done)], rows_out.at[:, pl.ds(0, done)], sem.at[1]),
+              pltpu.make_async_copy(end, rows_out.at[:, pl.ds(done, rows - done)], sem.at[2])]
+    copies[0].start()
+    copies[1].start()
+    more = nn(cd1[...], last[...])[:d, :]
+    end[...] = (rows_in[:, pl.ds(done, rows - done)] + more) * scale_r
+    copies[2].start()
     for cp in copies:
         cp.wait()
 
@@ -531,6 +539,7 @@
     dp = -(-(d + 6) // LANES) * LANES
     half = n // 2
     nq = rows // q_w
+    dq = -(-d // 16) * 16
     btiles = band // LANES
     cfg = (n, d, dp, w, band, rows, tile, q_w,
            1.0 / math.sqrt(w * n * lax.axis_size("col")), 1.0 / math.sqrt(rows * n))
@@ -543,7 +552,7 @@
         pltpu.VMEM((dp, rows), bf),
         pltpu.VMEM((w, dp), f32),
         pltpu.VMEM((2, n, w, dp), bf),
-        pltpu.VMEM((2, dp, band), bf),
+        pltpu.VMEM((dq, band), bf),
         pltpu.VMEM((2, nq, band, q_w), bf),
         pltpu.VMEM((nq, band, q_w), f32),
         pltpu.VMEM((nq, band, q_w), f32),
@@ -567,11 +576,12 @@
         pltpu.VMEM((2 * w, rows), bf),
     ]
     limit = min(60 << 20, (6 << 20) + scratch_bytes(scratch[:18]) + 2 * d * rows * 4 + 28 * band * q_w)
-    grad_rows, grad_cols = pl.pallas_call(
+    parts = pl.pallas_call(
         functools.partial(kernel, cfg),
-        out_shape=(jax.ShapeDtypeStruct((d, rows), f32), jax.ShapeDtypeStruct((w, d), f32)),
+        out_shape=(jax.ShapeDtypeStruct((d, rows), f32), jax.ShapeDtypeStruct((w, d), f32),
+                   jax.ShapeDtypeStruct((dq, band), bf), jax.ShapeDtypeStruct((band, q_w), bf)),
         in_specs=[hb] * 6 + [pl.BlockSpec(memory_space=pltpu.SMEM)],
-        out_specs=(vm, vm),
+        out_specs=(vm,) * 4,
         scratch_shapes=scratch,
         compiler_params=pltpu.CompilerParams(
             collective_id=0, has_side_effects=True, vmem_limit_bytes=limit),
@@ -587,12 +597,13 @@
         log_total,
     )
     grad_rows, grad_cols = pl.pallas_call(
-        place,
+        functools.partial(place, cfg[8]),
         out_shape=(jax.ShapeDtypeStruct((d, rows), f32), jax.ShapeDtypeStruct((w, d), f32)),
-        in_specs=[anywhere, anywhere],
+        in_specs=[vm] * 4,
         out_specs=(hb, hb),
-        scratch_shapes=[pltpu.SemaphoreType.DMA((2,))],
-    )(*(pltpu.with_memory_space_constraint(x, pltpu.VMEM) for x in (grad_rows, grad_cols)))
+        scratch_shapes=[pltpu.VMEM((d, q_w), f32), pltpu.SemaphoreType.DMA((3,))],
+        compiler_params=pltpu.CompilerParams(vmem_limit_bytes=limit),
+    )(*(pltpu.with_memory_space_constraint(x, pltpu.VMEM) for x in parts))
     return grad_rows, jnp.transpose(grad_cols.reshape(1, w, d), (2, 0, 1))
 
 

time: 19.7 us -> 19.5 us (0.990)
  Pallas kernels: 18.2 us -> 18 us
    pallas_call x1, Pallas kernels: 17.2 us -> 17 us  [body(): pl.pallas_call(functools.partial(kernel, cfg), out_shape=(jax.ShapeDtypeS...]
where the time goes in v4:
time: 19.5 us; the launch traced here: 19.3 us
  Pallas kernels  18 us (92%)
  between operations  1.29 us (7%)
    pallas_call x1, Pallas kernels, body(): pl.pallas_call(functools.partial(kernel, cfg), out_shape=(jax.ShapeDtypeS...  17 us
    pallas_call x1, Pallas kernels, body(): pl.pallas_call(functools.partial(place, cfg[8]), out_shape=(jax.ShapeDtyp...  1.07 us

profile of v4, /device:TPU:0, one launch (start us, length us, event | category | flops | bytes accessed | tf_op | source)
XLA Modules:
  0.0 19.3 jit_solution(1486604166769366575)
XLA Ops:
  1.3 17.0 %shard_map.86 = (f32[300,1024]{1,0:T(8,128)S(1)}, f32[16,300]{1,0:T(8,128)S(1)}, bf16[304,256]{1,0:T(8,128)(2,1)S(1)}, bf16[256,256]{1,0:T(8,128)(2,1)S(1)}) custom-call(bf16[300,1024]{1,0:T(8,128)(2,1)} %r_hbm.1, bf16[16,300]{1,0:T(8,128)(2,1)} %bitcast.12, s32[2048,128]{1,0:T(8,128)} %bitcast.11, s32[2,8]{1,0:T(2,128)} %bitcast.14, s32[1,1024]{1,0:T(1,128)} %bitcast.13, ...), custom_call_target="tpu_custom_call" | custom-call | tf_op jit(solution)/shard_map/pallas_call | solution.py:579
  18.2 1.1 %shard_map.87 = (f32[300,1024]{1,0:T(8,128)}, f32[16,300]{1,0:T(8,128)}) custom-call(f32[300,1024]{1,0:T(8,128)S(1)} %get-tuple-element.8.rows_in, f32[16,300]{1,0:T(8,128)S(1)} %get-tuple-element.9.cols_in, bf16[304,256]{1,0:T(8,128)(2,1)S(1)} %get-tuple-element.10.cd1, bf16[256,256]{1,0:T(8,128)(2,1)S(1)} %get-tuple-element.11.last), custom_call_target="tpu_custom_call" | custom-call | tf_op jit(solution)/shard_map/pallas_call | solution.py:599

commit v5 on v4

--- a/solution.py
+++ b/solution.py
@@ -53,7 +53,7 @@
            rows_out, cols_out, cd1, last,
            r_v, cnt_v, raug, blk, cg, cd0, enc, slope_v, logc_v, res, gcol, s1buf, s2src, s2buf,
            c_ref, occ_ref, rm_ref, cm_ref, dsem, e_s, e_r, gx_s, gx_r, g_s, g_r, w_s, w_r, m_s, m_r,
-           a_s, a_r, b_s, b_r, token, x_token, c_s, c_r, s0src, s0buf, res0):
+           a_s, a_r, b_s, b_r, token, x_token, c_s, c_r, h_s, h_r, s0src, s0buf, res0, spare):
     n, d, dp, w, band, rows, tile, q_w, scale_r, scale_c = cfg
     half = n // 2
     dq = -(-d // 16) * 16
@@ -184,6 +184,13 @@
         at = pl.ds(pl.multiple_of(part * gcols, gcols), gcols)
         rcopy(enc.at[0, q, at], enc.at[1, q, at], e_s, e_r.at[q], at_x).start()
 
+    def handed():
+        return rcopy(enc.at[0, nq - 2, pl.ds(gcols, gcols)], spare, h_s, h_r, at_mate)
+
+    def hand_on():
+        rcopy(spare, enc.at[1, nq - 2, pl.ds(gcols, gcols)], e_s, e_r.at[nq - 2],
+              (mate, 1 - col)).start()
+
     def x_starts(q):
         x_start(q, 0)
         x_start(q, 1)
@@ -258,7 +265,12 @@
     pl.when(mine < near)(lambda: to_far(0))
     rload.start()
     for q in range(2, nq):
-        x_starts(q - 1)
+        x_start(q - 1, 0)
+        if q == nq - 1:
+            pl.when(core == 1)(functools.partial(x_start, q - 1, 1))
+            pl.when(core == 0)(lambda: handed().start())
+        else:
+            x_start(q - 1, 1)
         encode(q)
 
     rload.wait()
@@ -322,9 +334,9 @@
             logc = both(lambda at: logc_v[q, at, :])
             res0[:, qs] = cell(code, slope, logc, gap).astype(jnp.bfloat16)
         s0src[...] = nt(res0[...], raug[...]).reshape(2, w, dp).astype(jnp.bfloat16)
-        spare = (mine - hh) * 2 + core
+        slot = (mine - hh) * 2 + core
         for c in range(2):
-            rcopy(s0src.at[c], s0buf.at[spare], c_s, c_r, (c, col)).start()
+            rcopy(s0src.at[c], s0buf.at[slot], c_s, c_r, (c, col)).start()
 
     def block(which, first, count):
         return cg[which, pl.ds(first, count)].reshape(count * w, dp)
@@ -414,6 +426,12 @@
     to_earlier(1)
     to_near(1, False)
     gathered(0, 0)
+
+    @pl.when(core == 1)
+    def _():
+        handed().wait_recv()
+        hand_on()
+
     from_mate_blocks(0, 0)
     half_terms(own_half)
     from_mate(own_half).start()
@@ -499,7 +517,16 @@
 
     pl.when(mine < hh)(lambda: told(n))
     pl.when(mine >= hh)(lambda: told(n - 1))
-    rcopy(enc.at[0], enc.at[1], e_s, gx_r, at_x).wait_send()
+    def crossed(pieces):
+        some = cnt_v.at[pl.ds(0, pieces * gcols * q_w // (2 * LANES))]
+        rcopy(some, some, e_s, gx_r, at_x).wait_send()
+
+    @pl.when(core == 0)
+    def _():
+        crossed(2 * nq - 1)
+        handed().wait_send()
+
+    pl.when(core == 1)(lambda: crossed(2 * nq + 1))
     some = gcol.at[pl.ds(0, half)]
     rcopy(some, some, a_s, gx_r, at_mate).wait_send()
     pl.when(mine < hh)(lambda: summed(half - 1).wait_send())
@@ -570,10 +597,11 @@
         dma(), dma(2), dma(), dma(),
         pltpu.SemaphoreType.REGULAR((half // 2 + 1,)),
         pltpu.SemaphoreType.REGULAR,
-        dma(), dma(),
+        dma(), dma(), dma(), dma(),
         pltpu.VMEM((2, w, dp), bf),
         pltpu.VMEM((half, w, dp), bf),
         pltpu.VMEM((2 * w, rows), bf),
+        pltpu.VMEM((band // 2, q_w), bf),
     ]
     limit = min(60 << 20, (6 << 20) + scratch_bytes(scratch[:18]) + 2 * d * rows * 4 + 28 * band * q_w)
     parts = pl.pallas_call(

time: 19.5 us -> 19.1 us (0.979)
  Pallas kernels: 18 us -> 17.5 us
    pallas_call x1, Pallas kernels: 17 us -> 16.4 us  [body(): pl.pallas_call(functools.partial(kernel, cfg), out_shape=(jax.ShapeDtypeS...]
where the time goes in v5:
time: 19.1 us; the launch traced here: 18.8 us
  Pallas kernels  17.5 us (92%)
  between operations  1.29 us (7%)
    pallas_call x1, Pallas kernels, body(): pl.pallas_call(functools.partial(kernel, cfg), out_shape=(jax.ShapeDtypeS...  16.4 us
    pallas_call x1, Pallas kernels, body(): pl.pallas_call(functools.partial(place, cfg[8]), out_shape=(jax.ShapeDtyp...  1.07 us

profile of v5, /device:TPU:0, one launch (start us, length us, event | category | flops | bytes accessed | tf_op | source)
XLA Modules:
  0.0 18.8 jit_solution(10265634683107828121)
XLA Ops:
  1.3 16.4 %shard_map.86 = (f32[300,1024]{1,0:T(8,128)S(1)}, f32[16,300]{1,0:T(8,128)S(1)}, bf16[304,256]{1,0:T(8,128)(2,1)S(1)}, bf16[256,256]{1,0:T(8,128)(2,1)S(1)}) custom-call(bf16[300,1024]{1,0:T(8,128)(2,1)} %r_hbm.1, bf16[16,300]{1,0:T(8,128)(2,1)} %bitcast.12, s32[2048,128]{1,0:T(8,128)} %bitcast.11, s32[2,8]{1,0:T(2,128)} %bitcast.14, s32[1,1024]{1,0:T(1,128)} %bitcast.13, ...), custom_call_target="tpu_custom_call" | custom-call | tf_op jit(solution)/shard_map/pallas_call | solution.py:607
  17.7 1.1 %shard_map.87 = (f32[300,1024]{1,0:T(8,128)}, f32[16,300]{1,0:T(8,128)}) custom-call(f32[300,1024]{1,0:T(8,128)S(1)} %get-tuple-element.8.rows_in, f32[16,300]{1,0:T(8,128)S(1)} %get-tuple-element.9.cols_in, bf16[304,256]{1,0:T(8,128)(2,1)S(1)} %get-tuple-element.10.cd1, bf16[256,256]{1,0:T(8,128)(2,1)S(1)} %get-tuple-element.11.last), custom_call_target="tpu_custom_call" | custom-call | tf_op jit(solution)/shard_map/pallas_call | solution.py:627

commit v6 on v5

--- a/solution.py
+++ b/solution.py
@@ -52,8 +52,8 @@
 def kernel(cfg, r_hbm, c_hbm, cnt_hbm, occ_hbm, rm_hbm, cm_hbm, lt_ref,
            rows_out, cols_out, cd1, last,
            r_v, cnt_v, raug, blk, cg, cd0, enc, slope_v, logc_v, res, gcol, s1buf, s2src, s2buf,
-           c_ref, occ_ref, rm_ref, cm_ref, dsem, e_s, e_r, gx_s, gx_r, g_s, g_r, w_s, w_r, m_s, m_r,
-           a_s, a_r, b_s, b_r, token, x_token, c_s, c_r, h_s, h_r, s0src, s0buf, res0, spare):
+           c_ref, occ_ref, rm_ref, cm_ref, dsem, e_s, e_r, gx_r, g_s, g_r, w_s, w_r, m_s, m_r,
+           a_s, a_r, b_s, b_r, token, x_token, c_r, h_r, s0src, s0buf, res0, spare):
     n, d, dp, w, band, rows, tile, q_w, scale_r, scale_c = cfg
     half = n // 2
     dq = -(-d // 16) * 16
@@ -107,12 +107,6 @@
     n_earlier = jnp.where(mine == 1, 2, jnp.where(mine == 2, 1, mine))
     n_far = jnp.where(mine < near, half - near, half - 1 - mine)
 
-    barrier = pltpu.get_barrier_semaphore()
-    pl.when(col == 0)(lambda: signal(barrier, at_x))
-    signal(barrier, at_mate)
-    each(later, lambda k: signal(barrier, at_peer(k)))
-    each(far_later, lambda k: signal(barrier, at_peer(k)))
-
     small = []
     step = q_w * btiles
     loads = [pltpu.make_async_copy(
@@ -121,18 +115,24 @@
     loads[0].start()
     for k, (src, dst) in enumerate(((cm_hbm, cm_ref), (c_hbm, c_ref), (occ_hbm, occ_ref),
                                     (rm_hbm, rm_ref))):
-        cp = pltpu.make_async_copy(src, dst, dsem.at[nq + 1 + k])
+        cp = pltpu.make_async_copy(src, dst, dsem.at[nq + k])
         cp.start()
         small.append(cp)
     for cp in loads[1:]:
         cp.start()
-    rload = pltpu.make_async_copy(r_hbm, r_v, dsem.at[nq])
+    barrier = pltpu.get_barrier_semaphore()
+    pl.when(col == 0)(lambda: signal(barrier, at_x))
+    signal(barrier, at_mate)
+    each(later, lambda k: signal(barrier, at_peer(k)))
+    each(far_later, lambda k: signal(barrier, at_peer(k)))
+
+    rload = pltpu.make_async_copy(r_hbm, r_v, dsem.at[0])
 
     pl.semaphore_wait(barrier, 1 + col + n_earlier)
     slot = jnp.minimum(mine, near)
     pl.when(col == 1)(lambda: signal(x_token, at_x))
-    each(earlier, lambda k: signal(token.at[slot], at_peer(k)))
-    each(far_earlier, lambda k: signal(token.at[slot], at_peer(k)))
+    each(earlier, lambda k: signal(token.at[slot - 1], at_peer(k)))
+    each(far_earlier, lambda k: signal(token.at[slot - 1], at_peer(k)))
 
     for cp in small:
         cp.wait()
@@ -185,7 +185,7 @@
         rcopy(enc.at[0, q, at], enc.at[1, q, at], e_s, e_r.at[q], at_x).start()
 
     def handed():
-        return rcopy(enc.at[0, nq - 2, pl.ds(gcols, gcols)], spare, h_s, h_r, at_mate)
+        return rcopy(enc.at[0, nq - 2, pl.ds(gcols, gcols)], spare, e_s, h_r, at_mate)
 
     def hand_on():
         rcopy(spare, enc.at[1, nq - 2, pl.ds(gcols, gcols)], e_s, e_r.at[nq - 2],
@@ -196,12 +196,12 @@
         x_start(q, 1)
 
     ecopies = [rcopy(enc.at[0, q], enc.at[1, q], e_s, e_r.at[q], at_x) for q in range(nq)]
-    xcp = rcopy(cg.at[0, spot], cg.at[1, spot], gx_s, gx_r, at_x)
+    xcp = rcopy(cg.at[0, spot], cg.at[1, spot], g_s, gx_r, at_x)
 
     def to_near(which, waiting):
         def one(k):
             if waiting:
-                pl.semaphore_wait(token.at[k], 1)
+                pl.semaphore_wait(token.at[k - 1], 1)
             if k == 2:
                 rcopy(cg.at[which, spot], cg.at[which, spot], g_s, w_r.at[which],
                       at_peer(k)).start()
@@ -225,7 +225,7 @@
     def far_ready():
         @pl.when(n_far > 0)
         def _():
-            pl.semaphore_wait(token.at[near], n_far)
+            pl.semaphore_wait(token.at[near - 1], n_far)
 
     def relay(which):
         @pl.when(mine == 2)
@@ -336,7 +336,7 @@
         s0src[...] = nt(res0[...], raug[...]).reshape(2, w, dp).astype(jnp.bfloat16)
         slot = (mine - hh) * 2 + core
         for c in range(2):
-            rcopy(s0src.at[c], s0buf.at[slot], c_s, c_r, (c, col)).start()
+            rcopy(s0src.at[c], s0buf.at[slot], b_s, c_r, (c, col)).start()
 
     def block(which, first, count):
         return cg[which, pl.ds(first, count)].reshape(count * w, dp)
@@ -485,7 +485,7 @@
         total = blk[...]
         for k in range(1, hh):
             total = total + s2buf[k].astype(jnp.float32)
-        rcopy(s0buf, s0buf, c_s, c_r, at_mate).wait_recv()
+        rcopy(s0buf, s0buf, b_s, c_r, at_mate).wait_recv()
         for k in range(half):
             total = total + s0buf[k].astype(jnp.float32)
         cols_out[...] = (total * scale_c)[:, :d]
@@ -499,18 +499,17 @@
         cols_out[...] = (total * scale_c)[:, :d]
 
     def sent(blocks):
-        some = gcol.at[pl.ds(0, blocks)]
+        some = cg.at[0, pl.ds(0, blocks)]
         rcopy(some, some, g_s, gx_r, at_mate).wait_send()
 
-    pl.when(mine == 0)(lambda: sent(near - 1))
-    pl.when(mine != 0)(lambda: sent(half - 1))
+    pl.when(mine == 0)(lambda: sent(2 * near - 1))
+    pl.when(mine != 0)(lambda: sent(n - 1))
 
     @pl.when(mine == 2)
     def _():
         some = gcol.at[pl.ds(0, 3 * (half - near) // 2)]
         rcopy(some, some, w_s, gx_r, at_mate).wait_send()
 
-    xcp.wait_send()
     def told(blocks):
         some = cg.at[0, pl.ds(0, blocks)]
         rcopy(some, some, m_s, gx_r, at_mate).wait_send()
@@ -521,20 +520,12 @@
         some = cnt_v.at[pl.ds(0, pieces * gcols * q_w // (2 * LANES))]
         rcopy(some, some, e_s, gx_r, at_x).wait_send()
 
-    @pl.when(core == 0)
-    def _():
-        crossed(2 * nq - 1)
-        handed().wait_send()
-
+    pl.when(core == 0)(lambda: crossed(2 * nq))
     pl.when(core == 1)(lambda: crossed(2 * nq + 1))
     some = gcol.at[pl.ds(0, half)]
     rcopy(some, some, a_s, gx_r, at_mate).wait_send()
     pl.when(mine < hh)(lambda: summed(half - 1).wait_send())
-
-    @pl.when(mine >= hh)
-    def _():
-        summed(half - 2).wait_send()
-        rcopy(s0src, s0src, c_s, c_r, at_mate).wait_send()
+    pl.when(mine >= hh)(lambda: summed(half).wait_send())
 
 
 def scratch_bytes(shapes):
@@ -592,12 +583,12 @@
         pltpu.VMEM((occupancy.shape[2], occupancy.shape[0]), jnp.int32),
         pltpu.VMEM((1, rows), jnp.int32),
         pltpu.VMEM((1, w), jnp.int32),
-        dma(nq + 5),
-        dma(), dma(nq), dma(), dma(), dma(), dma(2, 2), dma(), dma(2), dma(), dma(2, 2),
+        dma(nq + 4),
+        dma(), dma(nq), dma(), dma(), dma(2, 2), dma(), dma(2), dma(), dma(2, 2),
         dma(), dma(2), dma(), dma(),
-        pltpu.SemaphoreType.REGULAR((half // 2 + 1,)),
+        pltpu.SemaphoreType.REGULAR((half // 2,)),
         pltpu.SemaphoreType.REGULAR,
-        dma(), dma(), dma(), dma(),
+        dma(), dma(),
         pltpu.VMEM((2, w, dp), bf),
         pltpu.VMEM((half, w, dp), bf),
         pltpu.VMEM((2 * w, rows), bf),

time: 19.1 us -> 19 us (level)
  the two profiles are of different devices: /device:TPU:0 before, /device:TPU:10 now
where the time goes in v6:
time: 19 us; the launch traced here: 18.8 us
  Pallas kernels  17.6 us (93%)
  between operations  1.29 us (7%)
    pallas_call x1, Pallas kernels, body(): pl.pallas_call(functools.partial(kernel, cfg), out_shape=(jax.ShapeDtypeS...  16.5 us
    pallas_call x1, Pallas kernels, body(): pl.pallas_call(functools.partial(place, cfg[8]), out_shape=(jax.ShapeDtyp...  1.07 us

profile of v6, /device:TPU:10, one launch (start us, length us, event | category | flops | bytes accessed | tf_op | source)
XLA Modules:
  0.0 18.8 jit_solution(6370564813860150603)
XLA Ops:
  1.3 16.5 %shard_map.86 = (f32[300,1024]{1,0:T(8,128)S(1)}, f32[16,300]{1,0:T(8,128)S(1)}, bf16[304,256]{1,0:T(8,128)(2,1)S(1)}, bf16[256,256]{1,0:T(8,128)(2,1)S(1)}) custom-call(bf16[300,1024]{1,0:T(8,128)(2,1)} %r_hbm.1, bf16[16,300]{1,0:T(8,128)(2,1)} %bitcast.12, s32[2048,128]{1,0:T(8,128)} %bitcast.11, s32[2,8]{1,0:T(2,128)} %bitcast.14, s32[1,1024]{1,0:T(1,128)} %bitcast.13, ...), custom_call_target="tpu_custom_call" | custom-call | tf_op jit(solution)/shard_map/pallas_call | solution.py:598
  17.8 1.1 %shard_map.87 = (f32[300,1024]{1,0:T(8,128)}, f32[16,300]{1,0:T(8,128)}) custom-call(f32[300,1024]{1,0:T(8,128)S(1)} %get-tuple-element.8.rows_in, f32[16,300]{1,0:T(8,128)S(1)} %get-tuple-element.9.cols_in, bf16[304,256]{1,0:T(8,128)(2,1)S(1)} %get-tuple-element.10.cd1, bf16[256,256]{1,0:T(8,128)(2,1)S(1)} %get-tuple-element.11.last), custom_call_target="tpu_custom_call" | custom-call | tf_op jit(solution)/shard_map/pallas_call | solution.py:618

commit v7 on v6

--- a/solution.py
+++ b/solution.py
@@ -370,9 +370,12 @@
 
         repeat(nsubg, terms)
 
+    turns = [0, 2, 1] + list(range(3, hh))
+
     def spread(h, own):
         from_mate(h).wait_recv()
-        for i in range(hh):
+        held = None
+        for i in turns:
             k = h * hh + i
             total = gcol[(h * 2 + core) * hh + i] + s1buf[k]
             s2src[k] = total.astype(s2src.dtype)
@@ -381,19 +384,21 @@
                 def _():
                     blk[...] = total
 
-            if i and own:
-                pl.when(mine != k - 1)(lambda: reduced(k - 1).start())
-            elif i == 1:
-                pl.when(mine < hh)(lambda: reduced(k - 1).start())
-            elif i:
-                reduced(k - 1).start()
-
-    def spread_last(h, own):
-        k = h * hh + hh - 1
+            if held is not None:
+                send_terms(h, held, own)
+            held = i
+
+    def send_terms(h, i, own):
+        k = h * hh + i
         if own:
             pl.when(mine != k)(lambda: reduced(k).start())
+        elif i:
+            reduced(k).start()
         else:
-            reduced(k).start()
+            pl.when(mine < hh)(lambda: reduced(k).start())
+
+    def spread_last(h, own):
+        send_terms(h, turns[-1], own)
 
     ident_d = eye(dp)
 

time: 19 us -> 19.1 us (level)
  the two profiles are of different devices: /device:TPU:10 before, /device:TPU:6 now
where the time goes in v7:
time: 19.1 us; the launch traced here: 18.9 us
  Pallas kernels  17.6 us (92%)
  between operations  1.29 us (7%)
    pallas_call x1, Pallas kernels, body(): pl.pallas_call(functools.partial(kernel, cfg), out_shape=(jax.ShapeDtypeS...  16.5 us
    pallas_call x1, Pallas kernels, body(): pl.pallas_call(functools.partial(place, cfg[8]), out_shape=(jax.ShapeDtyp...  1.07 us

profile of v7, /device:TPU:6, one launch (start us, length us, event | category | flops | bytes accessed | tf_op | source)
XLA Modules:
  0.0 18.9 jit_solution(15742070414652584996)
XLA Ops:
  1.3 16.5 %shard_map.86 = (f32[300,1024]{1,0:T(8,128)S(1)}, f32[16,300]{1,0:T(8,128)S(1)}, bf16[304,256]{1,0:T(8,128)(2,1)S(1)}, bf16[256,256]{1,0:T(8,128)(2,1)S(1)}) custom-call(bf16[300,1024]{1,0:T(8,128)(2,1)} %r_hbm.1, bf16[16,300]{1,0:T(8,128)(2,1)} %bitcast.12, s32[2048,128]{1,0:T(8,128)} %bitcast.11, s32[2,8]{1,0:T(2,128)} %bitcast.14, s32[1,1024]{1,0:T(1,128)} %bitcast.13, ...), custom_call_target="tpu_custom_call" | custom-call | tf_op jit(solution)/shard_map/pallas_call | solution.py:603
  17.8 1.1 %shard_map.87 = (f32[300,1024]{1,0:T(8,128)}, f32[16,300]{1,0:T(8,128)}) custom-call(f32[300,1024]{1,0:T(8,128)S(1)} %get-tuple-element.8.rows_in, f32[16,300]{1,0:T(8,128)S(1)} %get-tuple-element.9.cols_in, bf16[304,256]{1,0:T(8,128)(2,1)S(1)} %get-tuple-element.10.cd1, bf16[256,256]{1,0:T(8,128)(2,1)S(1)} %get-tuple-element.11.last), custom_call_target="tpu_custom_call" | custom-call | tf_op jit(solution)/shard_map/pallas_call | solution.py:623
